TPU v7x, 512 devices: a whole 4x4x16 slice. The times are simulated.
512 devices in a mesh: row: 8 (over z_lo), col: 16 (over x, y), layer: 4 (over z_hi, core).
Axes of the slice: x: 4, y: 4, z: 16 (z_hi: 2, z_lo: 8; z = z_hi * 8 + z_lo), core: 2. Of those that a mesh axis runs over, the one named last changes fastest.
Arguments:
- doubles_amplitude_tensor: float32 [2304, 2048], P('col', 'layer'), may hold values from -6 to 6
- integrals: float32 [8, 16, 4, 96, 2048], P('row', 'col', 'layer'), may hold values from -0.125 to 0.125
- incoming_residual: float32 [2304, 49152], P('col', ('row', 'layer')), may hold values from -6 to 6
Outputs:
- updated_residual: float32 [2304, 49152], P('col', ('row', 'layer'))
All inputs are finite; a program needn't handle non-finite values.
Results may differ from a plain program's by a relative error of at most 0.00005.
Values sent between devices are 32-bit elements; how exact they have to be, the bound alone decides.
No kernel may reach another device: no remote copies, remote signals or barrier semaphores. Data moves between devices by JAX's collectives and lax.ppermute only.
A program may use at most 64 MiB of HBM per device.

v0:
```python
import jax
import jax.numpy as jnp
from jax import lax
from jax.sharding import PartitionSpec as P


def regroup(integrals):
    local = integrals.reshape(1, integrals.shape[3], integrals.shape[4])
    return lax.all_to_all(local, "layer", split_axis=2, concat_axis=0, tiled=True)


def on_device(doubles_amplitude_tensor, integrals, incoming_residual):
    ij_rows = doubles_amplitude_tensor.shape[0]
    regrouped = regroup(integrals)[None]
    partial_ladder_value = jnp.einsum(
        "ic,nlkc->inlk",
        doubles_amplitude_tensor,
        lax.all_gather(regrouped, "col", axis=0, tiled=True),
        precision=lax.Precision.HIGHEST,
        preferred_element_type=jnp.float32,
    )
    summed = lax.psum_scatter(partial_ladder_value, "layer", scatter_dimension=2, tiled=True)
    return incoming_residual + summed.reshape(ij_rows, -1)


def solution(mesh):
    return jax.shard_map(
        on_device,
        mesh=mesh,
        in_specs=(
            P("col", "layer"),
            P("row", "col", "layer", None, None),
            P("col", ("row", "layer")),
        ),
        out_specs=P("col", ("row", "layer")),
        check_vma=False,
    )
```

profile of v0, /device:TPU:1, one launch (start us, length us, event | category | flops | bytes accessed | tf_op | source)
XLA Modules:
  0.0 565.8 jit_solution(12398285052435293716)
XLA Ops:
  6.5 0.0 copy-start
  6.5 0.0 all-gather.3.cloned.1.call-start
  6.5 1.5 copy.7
  8.1 43.3 %all_to_all.15 = f32[1,96,2048]{1,0,2:T(1,128)S(1)} all-to-all(f32[1,96,2048]{1,0,2:T(1,128)S(1)} %bitcast.24), channel_id=1, replica_groups=mesh['row'=8,'col'=16,'layer'=4] {'layer'}, dimensions={2} | all-to-all | bytes 1572864 | tf_op jit(solution)/shard_map/all_to_all | solution.py:9
  51.4 1.2 copy.8
  52.6 0.0 all-gather.3.cloned.1.call-update
  52.6 0.0 all-reduce.3.cloned.1.call-start
  52.6 128.7 %all-gather.3.cloned.1.call-done = f32[64,1,96,512]{3,2,1,0:T(8,128)} async-done(((f32[4,1,96,512]{3,2,1,0:T(8,128)}), f32[64,1,96,512]{3,2,1,0:T(8,128)}) %all-gather.3.cloned.1.call-update) | async-done | bytes 12582928 | tf_op jit(solution)/shard_map/all_gather | solution.py:18
  181.3 0.0 copy-done
  181.4 18.7 %fusion = f32[144,16,4,96]{3,0,2,1:T(8,128)} fusion(f32[144,512]{1,0:T(8,128)S(1)} %copy-done, f32[16,4,96,512]{3,2,1,0:T(8,128)} %bitcast.22), kind=kOutput, calls=%fused_computation | convolution fusion | flops 5435817984 | bytes 16416768 | tf_op jit(solution)/shard_map/ic,nlkc->inlk/dot_general | solution.py:15
  200.1 0.0 copy-start.1
  200.1 0.0 all-reduce.3.cloned.1.call-update
  200.1 1.3 dynamic-slice
  201.5 353.6 %all-reduce.3.cloned.1.call-done = f32[144,16,4,96]{3,0,2,1:T(8,128)} async-done(((f32[144,16,4,96]{3,0,2,1:T(8,128)}), f32[144,16,4,96]{3,0,2,1:T(8,128)}) %all-reduce.3.cloned.1.call-update) | async-done | bytes 3538960
  555.1 2.0 constant_dynamic-slice_fusion
  557.1 0.4 copy.9
  557.5 0.5 reshape.8
  558.0 0.0 copy-done.1
  558.0 1.0 add.5
Async XLA Ops:
  6.5 174.8 %copy-start = (f32[144,512]{1,0:T(8,128)S(1)}, f32[144,512]{1,0:T(8,128)}, u32[]{:S(2)}) copy-start(f32[144,512]{1,0:T(8,128)} %param.3) | copy-start | bytes 884740
  6.5 174.8 %all-gather.3.cloned.1.call-start = ((), (), s32[]{:S(2)}) async-start(), calls=%async_computation.1 | async-start | bytes 13369344 | tf_op jit(solution)/shard_map/all_gather | solution.py:18
  52.6 502.5 %all-reduce.3.cloned.1.call-start = ((), (), s32[]{:S(2)}) async-start(), calls=%async_computation.2 | async-start | bytes 9437184
  200.1 357.9 %copy-start.1 = (f32[144,1536]{1,0:T(8,128)S(1)}, f32[144,1536]{1,0:T(8,128)}, u32[]{:S(2)}) copy-start(f32[144,1536]{1,0:T(8,128)} %param.5) | copy-start | bytes 2654212
Sparse Core Ops, SparseCore 0:
  52.7 128.5 all-gather.2
  200.2 354.7 all-reduce.2
where the time goes:
time: 566 us
  waiting for transfers between devices  482 us (85%)
  blocking collectives  43.3 us (8%)
  matrix products  18.7 us (3%)
  between operations  13.4 us (2%)
  local copies, waits for them, and re-layouts  6.95 us (1%)
    unnamed x3, waiting for transfers between devices  354 us
    all_gather x1, waiting for transfers between devices, on_device(): lax.all_gather(regrouped, 'col', axis=0, tiled=True)  129 us
    all_to_all x1, blocking collectives, regroup(): lax.all_to_all(local, 'layer', split_axis=2, concat_axis=0, tiled=True)  43.3 us
    dot_general x1, matrix products, on_device(): jnp.einsum('ic,nlkc->inlk', doubles_amplitude_tensor, lax.all_gather(regr...  18.7 us
  transfers between devices with their start and end apart: 2, of which 2 were waited for; matrix products, arithmetic and copies ran while one was open for 0% of the time, Pallas kernels for 0%

commit v1 on v0

v1 whole, which is shorter than its diff:
```python
import functools

import jax
import jax.numpy as jnp
from jax import lax
from jax.experimental import pallas as pl
from jax.experimental.pallas import tpu as pltpu
from jax.sharding import PartitionSpec as P

AXES = ("row", "col", "layer")
SIDE = 4
LIMIT = 24 * 2**20
FAKE = 30 * 10**9
PRICE = 20.0
GATE = 20 * 10**9


def device_of(x, y, z, core):
    return ((z % 8) * 16 + (x % 4) * 4 + y % 4) * 4 + (z % 16 // 8) * 2 + core


def shifted(dx=0, dz=0, swap=False):
    return [
        (device_of(x, y, z, core), device_of(x + dx, y, z + dz, 1 - core if swap else core))
        for x in range(4)
        for y in range(4)
        for z in range(16)
        for core in range(2)
    ]


Y_RINGS = [[x * SIDE + y for y in range(SIDE)] for x in range(SIDE)]
Y_RINGS_OF_TWO = [
    [(row + part) * 16 + x * SIDE + y for part in range(2) for y in range(SIDE)]
    for row in range(0, 8, 2)
    for x in range(SIDE)
]


def halves(value):
    high = value.astype(jnp.bfloat16)
    return high, (value - high.astype(jnp.float32)).astype(jnp.bfloat16)


def times(a, b):
    def one(p, q):
        return lax.dot_general(p, q, (((1,), (1,)), ((), ())), preferred_element_type=jnp.float32)

    (a_high, a_low), (b_high, b_low) = halves(a), halves(b)
    return one(a_high, b_high) + (one(a_high, b_low) + one(a_low, b_high))


def ladder_kernel(turns, accumulate, *refs):
    if accumulate:
        so_far, refs = refs[0], refs[1:]
    terms, blocks, out = refs[: len(turns)], refs[len(turns) : len(turns) + SIDE], refs[-1]
    layer = lax.axis_index("layer")
    ys, rows, _ = out.shape
    total = None
    for (far, swapped), t_ref in zip(turns, terms, strict=True):
        at_layer = ((layer // 2) ^ far) * 2 + ((layer % 2) ^ swapped)
        pieces, _, width = t_ref.shape
        at = pl.ds(pl.multiple_of(at_layer * width, width), width)
        v = jnp.concatenate([b[:, at] for b in blocks], axis=0)
        t = jnp.concatenate([t_ref[part * ys + y] for y in range(ys) for part in range(pieces // ys)], axis=0)
        total = times(t, v) if total is None else total + times(t, v)
    total = total.reshape(out.shape)
    out[...] = so_far[...] + total if accumulate else total


def ladder(turns, so_far, terms, blocks, shape, name, price=1.0, after=()):
    columns = sum(b.shape[0] for b in blocks)
    given = (() if so_far is None else (so_far,)) + (*terms, *blocks)
    flops = 2 * 3 * shape[0] * shape[1] * columns * len(turns) * terms[0].shape[-1]
    return pl.pallas_call(
        functools.partial(ladder_kernel, turns, so_far is not None),
        out_shape=jax.ShapeDtypeStruct(shape, jnp.float32),
        in_specs=[pl.BlockSpec(memory_space=pltpu.VMEM)] * len(given)
        + [pl.BlockSpec(memory_space=pl.ANY)] * len(after),
        out_specs=pl.BlockSpec(memory_space=pltpu.VMEM),
        cost_estimate=pl.CostEstimate(
            flops=int(flops * price),
            bytes_accessed=4 * sum(a.size for a in given) + 4 * shape[0] * shape[1] * shape[2],
            transcendentals=0,
        ),
        compiler_params=pltpu.CompilerParams(vmem_limit_bytes=LIMIT),
        name=name,
    )(*given, *after)


def gate_kernel(*refs):
    refs[-1][...] = jnp.zeros_like(refs[-1])


def gate(values, price):
    return pl.pallas_call(
        gate_kernel,
        out_shape=jax.ShapeDtypeStruct((8, 128), jnp.float32),
        in_specs=[pl.BlockSpec(memory_space=pl.ANY)] * len(values),
        out_specs=pl.BlockSpec(memory_space=pltpu.VMEM),
        cost_estimate=pl.CostEstimate(flops=price, bytes_accessed=4096, transcendentals=0),
        compiler_params=pltpu.CompilerParams(vmem_limit_bytes=LIMIT),
        name="arrived",
    )(*values)


def spread_kernel(given, out):
    for place in range(out.shape[0]):
        out[place] = given[...]


def spread(value, copies, name, price=0):
    return pl.pallas_call(
        spread_kernel,
        out_shape=jax.ShapeDtypeStruct((copies, *value.shape), jnp.float32),
        in_specs=[pl.BlockSpec(memory_space=pltpu.VMEM)],
        out_specs=pl.BlockSpec(memory_space=pltpu.VMEM),
        cost_estimate=pl.CostEstimate(
            flops=price, bytes_accessed=4 * value.size * (1 + copies), transcendentals=0
        ),
        compiler_params=pltpu.CompilerParams(vmem_limit_bytes=LIMIT),
        name=name,
    )(value)


def add_kernel(order, residual, parts, out):
    x = lax.axis_index("col") // SIDE
    ys, _, columns = parts.shape
    each = columns // SIDE
    for place, step in enumerate(order):
        at = pl.ds(pl.multiple_of((x + step) % SIDE * columns, columns), columns)
        block = jnp.concatenate([parts[y, :, place * each : (place + 1) * each] for y in range(ys)], axis=1)
        out[:, at] = residual[:, at] + block


def add(order, residual, parts):
    import functools

    return pl.pallas_call(
        functools.partial(add_kernel, order),
        out_shape=jax.ShapeDtypeStruct(residual.shape, jnp.float32),
        in_specs=[pl.BlockSpec(memory_space=pltpu.VMEM)] * 2,
        out_specs=pl.BlockSpec(memory_space=pltpu.VMEM),
        compiler_params=pltpu.CompilerParams(vmem_limit_bytes=LIMIT),
        name="add_ladder",
    )(residual, parts)


def on_device(t, integrals, residual):
    v = integrals.reshape(integrals.shape[3:])
    rows, width = t.shape

    def send(value, **move):
        return lax.ppermute(value, AXES, shifted(**move))

    def along_y(value):
        whole = spread(value, SIDE, "spread_near")
        return lax.all_to_all(whole, "col", 0, 0, axis_index_groups=Y_RINGS)

    def along_two(whole):
        return lax.all_to_all(whole, ("row", "col"), 0, 0, axis_index_groups=Y_RINGS_OF_TWO)

    share = lax.dynamic_slice_in_dim(t, lax.axis_index("row") % 2 * (rows // 2), rows // 2, 0)
    share_far = send(share, dz=8)
    v_left, v_right = send(v, dx=1), send(v, dx=-1)
    near = along_y(t)
    share_far = spread(share_far, 2 * SIDE, "spread_far", FAKE)
    share_far, v_left, v_right, v_next = lax.optimization_barrier((share_far, v_left, v_right, v))
    v_across = send(v_next, dx=2)
    near_pair = send(near, swap=True)
    far = along_two(share_far)
    order = (0, -1, 1, 2)
    blocks = (v, v_left, v_right, v_across)
    shape = (SIDE, rows, SIDE * v.shape[0])
    total = ladder(((0, 0), (0, 1)), None, (near, near_pair), blocks, shape, "ladder_near", PRICE, (gate((v_across,), GATE),))
    far, total = lax.optimization_barrier((far, total))
    far_pair = send(far, swap=True)
    total = ladder(((1, 0),), total, (far,), blocks, shape, "ladder_far")
    total = ladder(((1, 1),), total, (far_pair,), blocks, shape, "ladder_far_pair")
    parts = lax.all_to_all(total, "col", 0, 0, axis_index_groups=Y_RINGS)
    return add(order, residual, parts)


def solution(mesh):
    return jax.shard_map(
        on_device,
        mesh=mesh,
        in_specs=(
            P("col", "layer"),
            P("row", "col", "layer", None, None),
            P("col", ("row", "layer")),
        ),
        out_specs=P("col", ("row", "layer")),
        check_vma=False,
    )
```

time: 566 us -> 97.8 us (0.17)
  waiting for transfers between devices: 482 us -> 19.3 us
  starting transfers between devices: 0.04 us -> 42.6 us
  blocking collectives: 43.3 us -> 17.3 us
  matrix products: 18.7 us -> 0 us
  between operations: 13.4 us -> 0.13 us
  Pallas kernels: 0 us -> 11.2 us
    unnamed x3 -> x0, waiting for transfers between devices: 354 us -> none
    all_gather x1 -> x0, waiting for transfers between devices: 129 us -> none  [on_device(): lax.all_gather(regrouped, 'col', axis=0, tiled=True)]
    ppermute x0 -> x6, starting transfers between devices: none -> 33.9 us  [send(): return lax.ppermute(value, AXES, shifted(**move))]
    all_to_all x1, blocking collectives: 43.3 us -> 17.3 us  [on_device(): parts = lax.all_to_all(total, 'col', 0, 0, axis_index_groups=Y_RINGS)]
    ppermute x0 -> x6, waiting for transfers between devices: none -> 19.1 us  [send(): return lax.ppermute(value, AXES, shifted(**move))]
    dot_general x1 -> x0, matrix products: 18.7 us -> none  [on_device(): jnp.einsum('ic,nlkc->inlk', doubles_amplitude_tensor, lax.all_gather(regr...]
    pallas_call x0 -> x7, Pallas kernels: none -> 11.2 us  [the longest x3 7.67 us: ladder(): pl.pallas_call(functools.partial(ladder_kernel, turns, so_far is not None...]
    all_to_all x0 -> x2, starting transfers between devices: none -> 8.68 us  [the longest x1 4.5 us: along_two(): lax.all_to_all(whole, ('row', 'col'), 0, 0, axis_index_groups=Y_RINGS_OF_...]
  transfers between devices with their start and end apart: 2 -> 8, of which waited for: 2 -> 4; matrix products, arithmetic and copies ran while one was open for 0% -> 0% of each run, Pallas kernels for 0% -> 8%
where the time goes in v1:
time: 97.8 us; the launch traced here: 97.2 us
  starting transfers between devices  42.6 us (44%)
  waiting for transfers between devices  19.3 us (20%)
  blocking collectives  17.3 us (18%)
  Pallas kernels  11.2 us (11%)
  local copies, waits for them, and re-layouts  6.67 us (7%)
    ppermute x6, starting transfers between devices, send(): return lax.ppermute(value, AXES, shifted(**move))  33.9 us
    ppermute x6, waiting for transfers between devices, send(): return lax.ppermute(value, AXES, shifted(**move))  19.1 us
    all_to_all x1, blocking collectives, on_device(): parts = lax.all_to_all(total, 'col', 0, 0, axis_index_groups=Y_RINGS)  17.3 us
    pallas_call x3, Pallas kernels, ladder(): pl.pallas_call(functools.partial(ladder_kernel, turns, so_far is not None...  7.67 us
    unnamed x16, local copies, waits for them, and re-layouts  5.09 us
    all_to_all x1, starting transfers between devices, along_two(): lax.all_to_all(whole, ('row', 'col'), 0, 0, axis_index_groups=Y_RINGS_OF_...  4.5 us
    all_to_all x1, starting transfers between devices, along_y(): return lax.all_to_all(whole, 'col', 0, 0, axis_index_groups=Y_RINGS)  4.18 us
    pallas_call x2, Pallas kernels, spread(): pl.pallas_call(spread_kernel, out_shape=jax.ShapeDtypeStruct((copies, *va...  2.15 us
  transfers between devices with their start and end apart: 8, of which 4 were waited for; matrix products, arithmetic and copies ran while one was open for 0% of the time, Pallas kernels for 8%

profile of v1, /device:TPU:1, one launch (start us, length us, event | category | flops | bytes accessed | tf_op | source)
XLA Modules:
  0.0 97.2 jit_solution(3704982492485679522)
XLA Ops:
  0.0 1.6 %constant_dynamic-slice_fusion = f32[72,512]{1,0:T(8,128)} fusion(f32[144,512]{1,0:T(8,128)} %given.1, s32[]{:T(128)S(6)} %select_n.11), kind=kLoop, calls=%fused_computation | loop fusion | bytes 294916 | tf_op jit(solution)/shard_map/dynamic_slice | solution.py:163
  1.6 16.3 %collective-permute-start = (f32[72,512]{1,0:T(8,128)}, f32[72,512]{1,0:T(8,128)}, u32[]{:S(2)}, u32[]{:S(2)}) collective-permute-start(f32[72,512]{1,0:T(8,128)} %constant_dynamic-slice_fusion), channel_id=1, source_target_pairs={{0,2},{1,3},{64,66},{65,67},{128,130},{129,131},{192,194},{193,195... | collective-permute-start | bytes 442376 | tf_op jit(solution)/shard_map/ppermute | solution.py:154
  17.9 4.4 %collective-permute-start.2 = (f32[96,2048]{1,0:T(8,128)}, f32[96,2048]{1,0:T(8,128)S(1)}, u32[]{:S(2)}, u32[]{:S(2)}) collective-permute-start(f32[96,2048]{1,0:T(8,128)} %bitcast.1), channel_id=1, source_target_pairs={{0,48},{1,49},{64,112},{65,113},{128,176},{129,177},{192,240},{193... | collective-permute-start | bytes 2359304 | tf_op jit(solution)/shard_map/ppermute | solution.py:154
  22.2 1.9 %collective-permute-start.1 = (f32[96,2048]{1,0:T(8,128)}, f32[96,2048]{1,0:T(8,128)S(1)}, u32[]{:S(2)}, u32[]{:S(2)}) collective-permute-start(f32[96,2048]{1,0:T(8,128)} %bitcast.2), channel_id=1, source_target_pairs={{0,16},{1,17},{64,80},{65,81},{128,144},{129,145},{192,208},{193,2... | collective-permute-start | bytes 2359304 | tf_op jit(solution)/shard_map/ppermute | solution.py:154
  24.2 0.0 copy-start.7
  24.2 1.0 copy-done.7
  25.1 1.1 %spread_near.1 = f32[4,144,512]{2,1,0:T(8,128)} custom-call(f32[144,512]{1,0:T(8,128)S(1)} %copy-done.7), custom_call_target="tpu_custom_call" | custom-call | bytes 1474560 | tf_op jit(solution)/shard_map/spread_near/pallas_call | solution.py:113
  26.2 4.2 %all-to-all-start.1 = ((f32[4,144,512]{2,1,0:T(8,128)}), f32[4,144,512]{2,1,0:T(8,128)S(1)}, u32[]{:S(2)}, u32[]{:S(2)}) async-start(f32[4,144,512]{2,1,0:T(8,128)} %spread_near.1), calls=%async_computation.1 | async-start | bytes 2359296 | tf_op jit(solution)/shard_map/all_to_all | solution.py:158
  30.4 0.0 collective-permute-done.given
  30.4 1.1 %spread_far.1 = f32[8,72,512]{2,1,0:T(8,128)S(1)} custom-call(f32[72,512]{1,0:T(8,128)} %collective-permute-done.given), custom_call_target="tpu_custom_call" | custom-call | flops 30000001024 | bytes 1327104 | tf_op jit(solution)/shard_map/spread_far/pallas_call | solution.py:113
  31.5 1.0 %copy-done.3 = f32[8,72,512]{2,1,0:T(8,128)} copy-done((f32[8,72,512]{2,1,0:T(8,128)}, f32[8,72,512]{2,1,0:T(8,128)S(1)}, u32[]{:S(2)}) %copy-start.3) | copy-done | bytes 1179672
  32.5 5.9 %collective-permute-done.2.refs_4_ = f32[96,2048]{1,0:T(8,128)S(1)} collective-permute-done((f32[96,2048]{1,0:T(8,128)}, f32[96,2048]{1,0:T(8,128)S(1)}, u32[]{:S(2)}, u32[]{:S(2)}) %collective-permute-start.2) | collective-permute-done | bytes 786464 | tf_op jit(solution)/shard_map/ppermute | solution.py:154
  38.4 4.9 %collective-permute-done.1.refs_3_ = f32[96,2048]{1,0:T(8,128)S(1)} collective-permute-done((f32[96,2048]{1,0:T(8,128)}, f32[96,2048]{1,0:T(8,128)S(1)}, u32[]{:S(2)}, u32[]{:S(2)}) %collective-permute-start.1) | collective-permute-done | bytes 786464 | tf_op jit(solution)/shard_map/ppermute | solution.py:154
  43.4 1.9 %collective-permute-start.4 = (f32[96,2048]{1,0:T(8,128)S(1)}, f32[96,2048]{1,0:T(8,128)}, u32[]{:S(2)}, u32[]{:S(2)}) collective-permute-start(f32[96,2048]{1,0:T(8,128)S(1)} %bitcast.3), channel_id=1, source_target_pairs={{0,32},{1,33},{64,96},{65,97},{128,160},{129,161},{192,224},{193,2... | collective-permute-start | bytes 2359304 | tf_op jit(solution)/shard_map/ppermute | solution.py:154
  45.3 0.2 all-to-all-done.1.refs_0_
  45.4 1.0 %copy-done.1 = f32[4,144,512]{2,1,0:T(8,128)} copy-done((f32[4,144,512]{2,1,0:T(8,128)}, f32[4,144,512]{2,1,0:T(8,128)S(1)}, u32[]{:S(2)}) %copy-start.1) | copy-done | bytes 1179672
  46.5 4.5 %all-to-all-start = ((f32[8,72,512]{2,1,0:T(8,128)}), f32[8,72,512]{2,1,0:T(8,128)S(1)}, u32[]{:S(2)}, u32[]{:S(2)}) async-start(f32[8,72,512]{2,1,0:T(8,128)} %copy-done.3), calls=%async_computation | async-start | bytes 2359296 | tf_op jit(solution)/shard_map/all_to_all | solution.py:161
  51.0 4.5 %collective-permute-start.3 = (f32[4,144,512]{2,1,0:T(8,128)}, f32[4,144,512]{2,1,0:T(8,128)S(1)}, u32[]{:S(2)}, u32[]{:S(2)}) collective-permute-start(f32[4,144,512]{2,1,0:T(8,128)} %copy-done.1), channel_id=1, source_target_pairs={{0,1},{1,0},{64,65},{65,64},{128,129},{129,128},{192,193},{193,192... | collective-permute-start | bytes 3538952 | tf_op jit(solution)/shard_map/ppermute | solution.py:154
  55.5 8.3 %collective-permute-done.4.refs_0_.refs_5_ = f32[96,2048]{1,0:T(8,128)} collective-permute-done((f32[96,2048]{1,0:T(8,128)S(1)}, f32[96,2048]{1,0:T(8,128)}, u32[]{:S(2)}, u32[]{:S(2)}) %collective-permute-start.4) | collective-permute-done | bytes 786464 | tf_op jit(solution)/shard_map/ppermute | solution.py:154
  63.7 0.0 collective-permute-done.3.refs_1_
  63.7 3.2 %ladder_near.1.refs_0_ = f32[4,144,384]{2,1,0:T(8,128)S(1)} custom-call(f32[4,144,512]{2,1,0:T(8,128)S(1)} %copy-done.2, f32[4,144,512]{2,1,0:T(8,128)S(1)} %collective-permute-done.3.refs_1_, f32[96,2048]{1,0:T(8,128)S(1)} %bitcast.4, f32[96,2048]{1,0:T(8,128)S(1)} %collective-permute-done.1.refs_3_, f32[96,2048]{1,0:T(8,128)S(1)} %collective-permute-done.2.refs_4_, ...), custom_call_target="tpu_custom_call" | custom-call | flops 27179089920 | bytes 6389760 | tf_op jit(solution)/shard_map/ladder_near/pallas_call | solution.py:75
  66.9 0.0 copy-start.5
  66.9 0.9 copy-done.5
  67.8 0.0 all-to-all-done.refs_1_
  67.8 5.0 %collective-permute-start.5 = (f32[8,72,512]{2,1,0:T(8,128)S(1)}, f32[8,72,512]{2,1,0:T(8,128)S(1)}, u32[]{:S(2)}, u32[]{:S(2)}) collective-permute-start(f32[8,72,512]{2,1,0:T(8,128)S(1)} %all-to-all-done.refs_1_), channel_id=1, source_target_pairs={{0,1},{1,0},{64,65},{65,64},{128,129},{129,128},{192,193},{193,192... | collective-permute-start | bytes 3538952 | tf_op jit(solution)/shard_map/ppermute | solution.py:154
  72.8 0.0 copy-start.6
  72.8 1.2 %copy-done.6 = f32[4,144,384]{2,1,0:T(8,128)S(1)} copy-done((f32[4,144,384]{2,1,0:T(8,128)S(1)}, f32[4,144,384]{2,1,0:T(8,128)}, u32[]{:S(2)}) %copy-start.6) | copy-done | bytes 884760
  74.0 2.3 %ladder_far.1.refs_0_ = f32[4,144,384]{2,1,0:T(8,128)S(1)} custom-call(f32[4,144,384]{2,1,0:T(8,128)S(1)} %copy-done.6, f32[8,72,512]{2,1,0:T(8,128)S(1)} %all-to-all-done.refs_1_, f32[96,2048]{1,0:T(8,128)S(1)} %bitcast.5, f32[96,2048]{1,0:T(8,128)S(1)} %collective-permute-done.1.refs_3_, f32[96,2048]{1,0:T(8,128)S(1)} %collective-permute-done.2.refs_4_, ...), custom_call_target="tpu_custom_call" | custom-call | flops 679477248 | bytes 6094848 | tf_op jit(solution)/shard_map/ladder_far/pallas_call | solution.py:75
  76.3 2.3 %ladder_far_pair.1 = f32[4,144,384]{2,1,0:T(8,128)S(1)} custom-call(f32[4,144,384]{2,1,0:T(8,128)S(1)} %ladder_far.1.refs_0_, f32[8,72,512]{2,1,0:T(8,128)S(1)} %collective-permute-done.5.refs_1_, f32[96,2048]{1,0:T(8,128)S(1)} %bitcast.6, f32[96,2048]{1,0:T(8,128)S(1)} %collective-permute-done.1.refs_3_, f32[96,2048]{1,0:T(8,128)S(1)} %collective-permute-done.2.refs_4_, ...), custom_call_target="tpu_custom_call" | custom-call | flops 679477248 | bytes 6094848 | tf_op jit(solution)/shard_map/ladder_far_pair/pallas_call | solution.py:75
  78.5 0.0 copy-start.4
  78.5 17.3 %all_to_all.15.parts = f32[4,144,384]{2,1,0:T(8,128)S(1)} all-to-all(f32[4,144,384]{2,1,0:T(8,128)S(1)} %ladder_far_pair.1), channel_id=1, replica_groups={{0,4,8,12},{16,20,24,28},{32,36,40,44},{48,52,56,60},{1,5,9,13},{17,21,..., dimensions={0} | all-to-all | bytes 1769472 | tf_op jit(solution)/shard_map/all_to_all | solution.py:180
  95.8 1.3 %add_ladder.1 = f32[144,1536]{1,0:T(8,128)} custom-call(f32[144,1536]{1,0:T(8,128)S(1)} %copy-done.4, f32[4,144,384]{2,1,0:T(8,128)S(1)} %all_to_all.15.parts), custom_call_target="tpu_custom_call" | custom-call | tf_op jit(solution)/shard_map/add_ladder/pallas_call | solution.py:139
  (9 shorter events, 0.0 us)
Async XLA Ops:
  1.6 28.8 %collective-permute-start = (f32[72,512]{1,0:T(8,128)}, f32[72,512]{1,0:T(8,128)}, u32[]{:S(2)}, u32[]{:S(2)}) collective-permute-start(f32[72,512]{1,0:T(8,128)} %constant_dynamic-slice_fusion), channel_id=1, source_target_pairs={{0,2},{1,3},{64,66},{65,67},{128,130},{129,131},{192,194},{193,195... | collective-permute-start | bytes 442376 | tf_op jit(solution)/shard_map/ppermute | solution.py:154
  17.9 20.6 %collective-permute-start.2 = (f32[96,2048]{1,0:T(8,128)}, f32[96,2048]{1,0:T(8,128)S(1)}, u32[]{:S(2)}, u32[]{:S(2)}) collective-permute-start(f32[96,2048]{1,0:T(8,128)} %bitcast.1), channel_id=1, source_target_pairs={{0,48},{1,49},{64,112},{65,113},{128,176},{129,177},{192,240},{193... | collective-permute-start | bytes 2359304 | tf_op jit(solution)/shard_map/ppermute | solution.py:154
  22.2 21.1 %collective-permute-start.1 = (f32[96,2048]{1,0:T(8,128)}, f32[96,2048]{1,0:T(8,128)S(1)}, u32[]{:S(2)}, u32[]{:S(2)}) collective-permute-start(f32[96,2048]{1,0:T(8,128)} %bitcast.2), channel_id=1, source_target_pairs={{0,16},{1,17},{64,80},{65,81},{128,144},{129,145},{192,208},{193,2... | collective-permute-start | bytes 2359304 | tf_op jit(solution)/shard_map/ppermute | solution.py:154
  24.2 1.0 copy-start.7
  26.2 19.2 %all-to-all-start.1 = ((f32[4,144,512]{2,1,0:T(8,128)}), f32[4,144,512]{2,1,0:T(8,128)S(1)}, u32[]{:S(2)}, u32[]{:S(2)}) async-start(f32[4,144,512]{2,1,0:T(8,128)} %spread_near.1), calls=%async_computation.1 | async-start | bytes 2359296 | tf_op jit(solution)/shard_map/all_to_all | solution.py:158
  30.4 12.9 %copy-start = (f32[1,1,1,96,2048]{4,3,2,1,0:T(8,128)S(1)}, f32[1,1,1,96,2048]{4,3,2,1,0:T(8,128)}, u32[]{:S(2)}) copy-start(f32[1,1,1,96,2048]{4,3,2,1,0:T(8,128)} %param.4) | copy-start | bytes 2359300
  31.5 1.0 %copy-start.3 = (f32[8,72,512]{2,1,0:T(8,128)}, f32[8,72,512]{2,1,0:T(8,128)S(1)}, u32[]{:S(2)}) copy-start(f32[8,72,512]{2,1,0:T(8,128)S(1)} %spread_far.1) | copy-start | bytes 3538948
  43.4 20.4 %collective-permute-start.4 = (f32[96,2048]{1,0:T(8,128)S(1)}, f32[96,2048]{1,0:T(8,128)}, u32[]{:S(2)}, u32[]{:S(2)}) collective-permute-start(f32[96,2048]{1,0:T(8,128)S(1)} %bitcast.3), channel_id=1, source_target_pairs={{0,32},{1,33},{64,96},{65,97},{128,160},{129,161},{192,224},{193,2... | collective-permute-start | bytes 2359304 | tf_op jit(solution)/shard_map/ppermute | solution.py:154
  45.4 1.0 %copy-start.1 = (f32[4,144,512]{2,1,0:T(8,128)}, f32[4,144,512]{2,1,0:T(8,128)S(1)}, u32[]{:S(2)}) copy-start(f32[4,144,512]{2,1,0:T(8,128)S(1)} %all-to-all-done.1.refs_0_) | copy-start | bytes 3538948
  46.5 21.4 %all-to-all-start = ((f32[8,72,512]{2,1,0:T(8,128)}), f32[8,72,512]{2,1,0:T(8,128)S(1)}, u32[]{:S(2)}, u32[]{:S(2)}) async-start(f32[8,72,512]{2,1,0:T(8,128)} %copy-done.3), calls=%async_computation | async-start | bytes 2359296 | tf_op jit(solution)/shard_map/all_to_all | solution.py:161
  51.0 12.8 %copy-start.2 = (f32[4,144,512]{2,1,0:T(8,128)S(1)}, f32[4,144,512]{2,1,0:T(8,128)}, u32[]{:S(2)}) copy-start(f32[4,144,512]{2,1,0:T(8,128)} %copy-done.1) | copy-start | bytes 3538948
  51.0 12.8 %collective-permute-start.3 = (f32[4,144,512]{2,1,0:T(8,128)}, f32[4,144,512]{2,1,0:T(8,128)S(1)}, u32[]{:S(2)}, u32[]{:S(2)}) collective-permute-start(f32[4,144,512]{2,1,0:T(8,128)} %copy-done.1), channel_id=1, source_target_pairs={{0,1},{1,0},{64,65},{65,64},{128,129},{129,128},{192,193},{193,192... | collective-permute-start | bytes 3538952 | tf_op jit(solution)/shard_map/ppermute | solution.py:154
  66.9 0.9 copy-start.5
  67.8 8.4 %collective-permute-start.5 = (f32[8,72,512]{2,1,0:T(8,128)S(1)}, f32[8,72,512]{2,1,0:T(8,128)S(1)}, u32[]{:S(2)}, u32[]{:S(2)}) collective-permute-start(f32[8,72,512]{2,1,0:T(8,128)S(1)} %all-to-all-done.refs_1_), channel_id=1, source_target_pairs={{0,1},{1,0},{64,65},{65,64},{128,129},{129,128},{192,193},{193,192... | collective-permute-start | bytes 3538952 | tf_op jit(solution)/shard_map/ppermute | solution.py:154
  72.8 1.2 %copy-start.6 = (f32[4,144,384]{2,1,0:T(8,128)S(1)}, f32[4,144,384]{2,1,0:T(8,128)}, u32[]{:S(2)}) copy-start(f32[4,144,384]{2,1,0:T(8,128)} %copy-done.5) | copy-start | bytes 2654212
  78.5 17.3 %copy-start.4 = (f32[144,1536]{1,0:T(8,128)S(1)}, f32[144,1536]{1,0:T(8,128)}, u32[]{:S(2)}) copy-start(f32[144,1536]{1,0:T(8,128)} %residual.1) | copy-start | bytes 2654212

commit v2 on v1

--- a/solution.py
+++ b/solution.py
@@ -10,18 +10,21 @@
 AXES = ("row", "col", "layer")
 SIDE = 4
 LIMIT = 24 * 2**20
-FAKE = 30 * 10**9
+FAKE = 12 * 10**9
 PRICE = 20.0
-GATE = 20 * 10**9
+GATE = 10 * 10**9
 
 
 def device_of(x, y, z, core):
     return ((z % 8) * 16 + (x % 4) * 4 + y % 4) * 4 + (z % 16 // 8) * 2 + core
 
 
-def shifted(dx=0, dz=0, swap=False):
+def shifted(dx=0, mirror=False, swap=False):
     return [
-        (device_of(x, y, z, core), device_of(x + dx, y, z + dz, 1 - core if swap else core))
+        (
+            device_of(x, y, z, core),
+            device_of(x + dx, y, 15 - z if mirror else z, 1 - core if swap else core),
+        )
         for x in range(4)
         for y in range(4)
         for z in range(16)
@@ -50,10 +53,10 @@
     return one(a_high, b_high) + (one(a_high, b_low) + one(a_low, b_high))
 
 
-def ladder_kernel(turns, accumulate, *refs):
+def ladder_kernel(turns, accumulate, n_blocks, *refs):
     if accumulate:
         so_far, refs = refs[0], refs[1:]
-    terms, blocks, out = refs[: len(turns)], refs[len(turns) : len(turns) + SIDE], refs[-1]
+    terms, blocks, out = refs[: len(turns)], refs[len(turns) : len(turns) + n_blocks], refs[-1]
     layer = lax.axis_index("layer")
     ys, rows, _ = out.shape
     total = None
@@ -69,11 +72,10 @@
 
 
 def ladder(turns, so_far, terms, blocks, shape, name, price=1.0, after=()):
-    columns = sum(b.shape[0] for b in blocks)
     given = (() if so_far is None else (so_far,)) + (*terms, *blocks)
-    flops = 2 * 3 * shape[0] * shape[1] * columns * len(turns) * terms[0].shape[-1]
-    return pl.pallas_call(
-        functools.partial(ladder_kernel, turns, so_far is not None),
+    flops = 2 * 3 * shape[0] * shape[1] * shape[2] * len(turns) * terms[0].shape[-1]
+    return pl.pallas_call(
+        functools.partial(ladder_kernel, turns, so_far is not None, len(blocks)),
         out_shape=jax.ShapeDtypeStruct(shape, jnp.float32),
         in_specs=[pl.BlockSpec(memory_space=pltpu.VMEM)] * len(given)
         + [pl.BlockSpec(memory_space=pl.ANY)] * len(after),
@@ -104,9 +106,12 @@
     )(*values)
 
 
-def spread_kernel(given, out):
-    for place in range(out.shape[0]):
-        out[place] = given[...]
+def spread_kernel(given, whole, sems):
+    copies = [pltpu.make_async_copy(given, whole.at[k], sems.at[k]) for k in range(whole.shape[0])]
+    for copy in copies:
+        copy.start()
+    for copy in copies:
+        copy.wait()
 
 
 def spread(value, copies, name, price=0):
@@ -114,13 +119,36 @@
         spread_kernel,
         out_shape=jax.ShapeDtypeStruct((copies, *value.shape), jnp.float32),
         in_specs=[pl.BlockSpec(memory_space=pltpu.VMEM)],
-        out_specs=pl.BlockSpec(memory_space=pltpu.VMEM),
+        out_specs=pl.BlockSpec(memory_space=pltpu.HBM),
+        scratch_shapes=[pltpu.SemaphoreType.DMA((copies,))],
         cost_estimate=pl.CostEstimate(
             flops=price, bytes_accessed=4 * value.size * (1 + copies), transcendentals=0
         ),
         compiler_params=pltpu.CompilerParams(vmem_limit_bytes=LIMIT),
         name=name,
     )(value)
+
+
+def share_kernel(t, out, sem):
+    rows = out.shape[0]
+    at = pl.ds(pl.multiple_of((1 - lax.axis_index("row") % 2) * rows, 8), rows)
+    copy = pltpu.make_async_copy(t.at[at], out, sem)
+    copy.start()
+    copy.wait()
+
+
+def share_of(t):
+    rows, width = t.shape
+    return pl.pallas_call(
+        share_kernel,
+        out_shape=jax.ShapeDtypeStruct((rows // 2, width), jnp.float32),
+        in_specs=[pl.BlockSpec(memory_space=pl.ANY)],
+        out_specs=pl.BlockSpec(memory_space=pltpu.VMEM),
+        scratch_shapes=[pltpu.SemaphoreType.DMA],
+        cost_estimate=pl.CostEstimate(flops=0, bytes_accessed=4 * t.size, transcendentals=0),
+        compiler_params=pltpu.CompilerParams(vmem_limit_bytes=LIMIT),
+        name="share",
+    )(t)
 
 
 def add_kernel(order, residual, parts, out):
@@ -148,31 +176,24 @@
 
 def on_device(t, integrals, residual):
     v = integrals.reshape(integrals.shape[3:])
-    rows, width = t.shape
+    rows = t.shape[0]
 
     def send(value, **move):
         return lax.ppermute(value, AXES, shifted(**move))
 
-    def along_y(value):
-        whole = spread(value, SIDE, "spread_near")
-        return lax.all_to_all(whole, "col", 0, 0, axis_index_groups=Y_RINGS)
-
-    def along_two(whole):
-        return lax.all_to_all(whole, ("row", "col"), 0, 0, axis_index_groups=Y_RINGS_OF_TWO)
-
-    share = lax.dynamic_slice_in_dim(t, lax.axis_index("row") % 2 * (rows // 2), rows // 2, 0)
-    share_far = send(share, dz=8)
+    share_far = send(share_of(t), mirror=True)
     v_left, v_right = send(v, dx=1), send(v, dx=-1)
-    near = along_y(t)
-    share_far = spread(share_far, 2 * SIDE, "spread_far", FAKE)
-    share_far, v_left, v_right, v_next = lax.optimization_barrier((share_far, v_left, v_right, v))
+    near = lax.all_to_all(spread(t, SIDE, "spread_near"), "col", 0, 0, axis_index_groups=Y_RINGS)
+    v_left, v_right, v_next = lax.optimization_barrier((v_left, v_right, v))
     v_across = send(v_next, dx=2)
+    far = spread(share_far, 2 * SIDE, "spread_far", FAKE)
+    far = lax.all_to_all(far, ("row", "col"), 0, 0, axis_index_groups=Y_RINGS_OF_TWO)
     near_pair = send(near, swap=True)
-    far = along_two(share_far)
     order = (0, -1, 1, 2)
     blocks = (v, v_left, v_right, v_across)
     shape = (SIDE, rows, SIDE * v.shape[0])
-    total = ladder(((0, 0), (0, 1)), None, (near, near_pair), blocks, shape, "ladder_near", PRICE, (gate((v_across,), GATE),))
+    arrived = (gate((v_across,), GATE),)
+    total = ladder(((0, 0), (0, 1)), None, (near, near_pair), blocks, shape, "ladder_near", PRICE, arrived)
     far, total = lax.optimization_barrier((far, total))
     far_pair = send(far, swap=True)
     total = ladder(((1, 0),), total, (far,), blocks, shape, "ladder_far")

time: 97.8 us -> 87.8 us (0.90)
  waiting for transfers between devices: 19.3 us -> 11.4 us
  Pallas kernels: 11.2 us -> 13.4 us
  local copies, waits for them, and re-layouts: 6.67 us -> 5.09 us
  starting transfers between devices: 42.6 us -> 41.1 us
  blocking collectives: 17.3 us -> 16 us
    ppermute x6, waiting for transfers between devices: 19.1 us -> 7.35 us  [send(): return lax.ppermute(value, AXES, shifted(**move))]
    all_to_all x2, waiting for transfers between devices: 0.16 us -> 4.04 us  [the longest x1 3.17 us: on_device(): lax.all_to_all(spread(t, SIDE, 'spread_near'), 'col', 0, 0, axis_index_gr...]
    dynamic_slice x1 -> x0, local copies, waits for them, and re-layouts: 1.58 us -> none  [on_device(): lax.dynamic_slice_in_dim(t, lax.axis_index('row') % 2 * (rows // 2), rows...]
    pallas_call x2, Pallas kernels: 2.15 us -> 3.55 us  [spread(): pl.pallas_call(spread_kernel, out_shape=jax.ShapeDtypeStruct((copies, *va...]
    all_to_all x1, blocking collectives: 17.3 us -> 16 us  [on_device(): parts = lax.all_to_all(total, 'col', 0, 0, axis_index_groups=Y_RINGS)]
  transfers between devices with their start and end apart: 8 -> 8, of which waited for: 4 -> 4; matrix products, arithmetic and copies ran while one was open for 0% -> 0% of each run, Pallas kernels for 8% -> 11%
where the time goes in v2:
time: 87.8 us; the launch traced here: 87.2 us
  starting transfers between devices  41.1 us (47%)
  blocking collectives  16 us (18%)
  Pallas kernels  13.4 us (15%)
  waiting for transfers between devices  11.4 us (13%)
  local copies, waits for them, and re-layouts  5.09 us (6%)
    ppermute x6, starting transfers between devices, send(): return lax.ppermute(value, AXES, shifted(**move))  33.2 us
    all_to_all x1, blocking collectives, on_device(): parts = lax.all_to_all(total, 'col', 0, 0, axis_index_groups=Y_RINGS)  16 us
    pallas_call x3, Pallas kernels, ladder(): pl.pallas_call(functools.partial(ladder_kernel, turns, so_far is not None...  7.67 us
    ppermute x6, waiting for transfers between devices, send(): return lax.ppermute(value, AXES, shifted(**move))  7.35 us
    unnamed x16, local copies, waits for them, and re-layouts  5.09 us
    all_to_all x1, starting transfers between devices, on_device(): lax.all_to_all(spread(t, SIDE, 'spread_near'), 'col', 0, 0, axis_index_gr...  4.33 us
    all_to_all x1, starting transfers between devices, on_device(): lax.all_to_all(far, ('row', 'col'), 0, 0, axis_index_groups=Y_RINGS_OF_TWO)  3.56 us
    pallas_call x2, Pallas kernels, spread(): pl.pallas_call(spread_kernel, out_shape=jax.ShapeDtypeStruct((copies, *va...  3.55 us
  transfers between devices with their start and end apart: 8, of which 4 were waited for; matrix products, arithmetic and copies ran while one was open for 0% of the time, Pallas kernels for 11%

profile of v2, /device:TPU:1, one launch (start us, length us, event | category | flops | bytes accessed | tf_op | source)
XLA Modules:
  0.0 87.2 jit_solution(13352559688218743133)
XLA Ops:
  0.0 3.9 %collective-permute-start.2 = (f32[96,2048]{1,0:T(8,128)}, f32[96,2048]{1,0:T(8,128)S(1)}, u32[]{:S(2)}, u32[]{:S(2)}) collective-permute-start(f32[96,2048]{1,0:T(8,128)} %bitcast.1), channel_id=1, source_target_pairs={{0,16},{1,17},{64,80},{65,81},{128,144},{129,145},{192,208},{193,2... | collective-permute-start | bytes 2359304 | tf_op jit(solution)/shard_map/ppermute | solution.py:182
  3.9 3.2 %collective-permute-start.3 = (f32[96,2048]{1,0:T(8,128)}, f32[96,2048]{1,0:T(8,128)S(1)}, u32[]{:S(2)}, u32[]{:S(2)}) collective-permute-start(f32[96,2048]{1,0:T(8,128)} %bitcast.2), channel_id=1, source_target_pairs={{0,48},{1,49},{64,112},{65,113},{128,176},{129,177},{192,240},{193... | collective-permute-start | bytes 2359304 | tf_op jit(solution)/shard_map/ppermute | solution.py:182
  7.2 1.0 %copy-done.4 = f32[144,512]{1,0:T(8,128)S(1)} copy-done((f32[144,512]{1,0:T(8,128)S(1)}, f32[144,512]{1,0:T(8,128)}, u32[]{:S(2)}) %copy-start.4) | copy-done | bytes 294936
  8.1 0.8 share.1
  8.9 11.3 %collective-permute-start = (f32[72,512]{1,0:T(8,128)}, f32[72,512]{1,0:T(8,128)}, u32[]{:S(2)}, u32[]{:S(2)}) collective-permute-start(f32[72,512]{1,0:T(8,128)} %share.1), channel_id=1, source_target_pairs={{0,450},{1,451},{64,386},{65,387},{128,322},{129,323},{192,258},{1... | collective-permute-start | bytes 442376 | tf_op jit(solution)/shard_map/ppermute | solution.py:182
  20.3 1.1 %spread_near.1 = f32[4,144,512]{2,1,0:T(8,128)} custom-call(f32[144,512]{1,0:T(8,128)S(1)} %copy-done.4), custom_call_target="tpu_custom_call" | custom-call | bytes 1474560 | tf_op jit(solution)/shard_map/spread_near/pallas_call | solution.py:118
  21.4 0.0 copy-start
  21.4 4.3 %all-to-all-start.1 = ((f32[4,144,512]{2,1,0:T(8,128)}), f32[4,144,512]{2,1,0:T(8,128)S(1)}, u32[]{:S(2)}, u32[]{:S(2)}) async-start(f32[4,144,512]{2,1,0:T(8,128)} %spread_near.1), calls=%async_computation.1 | async-start | bytes 2359296 | tf_op jit(solution)/shard_map/all_to_all | solution.py:186
  25.7 0.0 collective-permute-done.2.refs_3_
  25.7 3.4 %collective-permute-start.4 = (f32[96,2048]{1,0:T(8,128)S(1)}, f32[96,2048]{1,0:T(8,128)}, u32[]{:S(2)}, u32[]{:S(2)}) collective-permute-start(f32[96,2048]{1,0:T(8,128)S(1)} %bitcast.3), channel_id=1, source_target_pairs={{0,32},{1,33},{64,96},{65,97},{128,160},{129,161},{192,224},{193,2... | collective-permute-start | bytes 2359304 | tf_op jit(solution)/shard_map/ppermute | solution.py:182
  29.2 4.7 %collective-permute-done.given = f32[72,512]{1,0:T(8,128)} collective-permute-done((f32[72,512]{1,0:T(8,128)}, f32[72,512]{1,0:T(8,128)}, u32[]{:S(2)}, u32[]{:S(2)}) %collective-permute-start) | collective-permute-done | bytes 147488 | tf_op jit(solution)/shard_map/ppermute | solution.py:182
  33.9 2.5 %spread_far.1 = f32[8,72,512]{2,1,0:T(8,128)S(1)} custom-call(f32[72,512]{1,0:T(8,128)} %collective-permute-done.given), custom_call_target="tpu_custom_call" | custom-call | flops 12000000000 | bytes 1327104 | tf_op jit(solution)/shard_map/spread_far/pallas_call | solution.py:118
  36.3 1.0 %copy-done.3 = f32[8,72,512]{2,1,0:T(8,128)} copy-done((f32[8,72,512]{2,1,0:T(8,128)}, f32[8,72,512]{2,1,0:T(8,128)S(1)}, u32[]{:S(2)}) %copy-start.3) | copy-done | bytes 1179672
  37.4 3.2 %all-to-all-done.1.refs_0_ = f32[4,144,512]{2,1,0:T(8,128)S(1)} async-done(((f32[4,144,512]{2,1,0:T(8,128)}), f32[4,144,512]{2,1,0:T(8,128)S(1)}, u32[]{:S(2)}, u32[]{:S(2)}) %all-to-all-start.1) | async-done | bytes 1179680 | tf_op jit(solution)/shard_map/all_to_all | solution.py:186
  40.5 1.0 %copy-done.1 = f32[4,144,512]{2,1,0:T(8,128)} copy-done((f32[4,144,512]{2,1,0:T(8,128)}, f32[4,144,512]{2,1,0:T(8,128)S(1)}, u32[]{:S(2)}) %copy-start.1) | copy-done | bytes 1179672
  41.6 3.6 %all-to-all-start = ((f32[8,72,512]{2,1,0:T(8,128)}), f32[8,72,512]{2,1,0:T(8,128)S(1)}, u32[]{:S(2)}, u32[]{:S(2)}) async-start(f32[8,72,512]{2,1,0:T(8,128)} %copy-done.3), calls=%async_computation | async-start | bytes 2359296 | tf_op jit(solution)/shard_map/all_to_all | solution.py:190
  45.2 4.9 %collective-permute-start.1 = (f32[4,144,512]{2,1,0:T(8,128)}, f32[4,144,512]{2,1,0:T(8,128)S(1)}, u32[]{:S(2)}, u32[]{:S(2)}) collective-permute-start(f32[4,144,512]{2,1,0:T(8,128)} %copy-done.1), channel_id=1, source_target_pairs={{0,1},{1,0},{64,65},{65,64},{128,129},{129,128},{192,193},{193,192... | collective-permute-start | bytes 3538952 | tf_op jit(solution)/shard_map/ppermute | solution.py:182
  50.0 0.0 collective-permute-done.4.refs_0_.refs_5_
  50.0 2.6 %collective-permute-done.1.refs_1_ = f32[4,144,512]{2,1,0:T(8,128)S(1)} collective-permute-done((f32[4,144,512]{2,1,0:T(8,128)}, f32[4,144,512]{2,1,0:T(8,128)S(1)}, u32[]{:S(2)}, u32[]{:S(2)}) %collective-permute-start.1) | collective-permute-done | bytes 1179680 | tf_op jit(solution)/shard_map/ppermute | solution.py:182
  52.7 3.2 %ladder_near.1.refs_0_ = f32[4,144,384]{2,1,0:T(8,128)S(1)} custom-call(f32[4,144,512]{2,1,0:T(8,128)S(1)} %copy-done.2, f32[4,144,512]{2,1,0:T(8,128)S(1)} %collective-permute-done.1.refs_1_, f32[96,2048]{1,0:T(8,128)S(1)} %bitcast.4, f32[96,2048]{1,0:T(8,128)S(1)} %collective-permute-done.2.refs_3_, f32[96,2048]{1,0:T(8,128)S(1)} %collective-permute-done.3.refs_4_, ...), custom_call_target="tpu_custom_call" | custom-call | flops 27179089920 | bytes 6389760 | tf_op jit(solution)/shard_map/ladder_near/pallas_call | solution.py:77
  55.9 0.0 copy-start.6
  55.9 0.9 %copy-done.6 = f32[4,144,384]{2,1,0:T(8,128)} copy-done((f32[4,144,384]{2,1,0:T(8,128)}, f32[4,144,384]{2,1,0:T(8,128)S(1)}, u32[]{:S(2)}) %copy-start.6) | copy-done | bytes 884760
  56.8 0.9 all-to-all-done.refs_1_
  57.6 6.5 %collective-permute-start.5 = (f32[8,72,512]{2,1,0:T(8,128)S(1)}, f32[8,72,512]{2,1,0:T(8,128)S(1)}, u32[]{:S(2)}, u32[]{:S(2)}) collective-permute-start(f32[8,72,512]{2,1,0:T(8,128)S(1)} %all-to-all-done.refs_1_), channel_id=1, source_target_pairs={{0,1},{1,0},{64,65},{65,64},{128,129},{129,128},{192,193},{193,192... | collective-permute-start | bytes 3538952 | tf_op jit(solution)/shard_map/ppermute | solution.py:182
  64.1 0.0 copy-start.7
  64.2 1.2 %copy-done.7 = f32[4,144,384]{2,1,0:T(8,128)S(1)} copy-done((f32[4,144,384]{2,1,0:T(8,128)S(1)}, f32[4,144,384]{2,1,0:T(8,128)}, u32[]{:S(2)}) %copy-start.7) | copy-done | bytes 884760
  65.3 2.3 %ladder_far.1.refs_0_ = f32[4,144,384]{2,1,0:T(8,128)S(1)} custom-call(f32[4,144,384]{2,1,0:T(8,128)S(1)} %copy-done.7, f32[8,72,512]{2,1,0:T(8,128)S(1)} %all-to-all-done.refs_1_, f32[96,2048]{1,0:T(8,128)S(1)} %bitcast.5, f32[96,2048]{1,0:T(8,128)S(1)} %collective-permute-done.2.refs_3_, f32[96,2048]{1,0:T(8,128)S(1)} %collective-permute-done.3.refs_4_, ...), custom_call_target="tpu_custom_call" | custom-call | flops 679477248 | bytes 6094848 | tf_op jit(solution)/shard_map/ladder_far/pallas_call | solution.py:77
  67.6 0.0 collective-permute-done.5.refs_1_
  67.6 2.3 %ladder_far_pair.1 = f32[4,144,384]{2,1,0:T(8,128)S(1)} custom-call(f32[4,144,384]{2,1,0:T(8,128)S(1)} %ladder_far.1.refs_0_, f32[8,72,512]{2,1,0:T(8,128)S(1)} %collective-permute-done.5.refs_1_, f32[96,2048]{1,0:T(8,128)S(1)} %bitcast.6, f32[96,2048]{1,0:T(8,128)S(1)} %collective-permute-done.2.refs_3_, f32[96,2048]{1,0:T(8,128)S(1)} %collective-permute-done.3.refs_4_, ...), custom_call_target="tpu_custom_call" | custom-call | flops 679477248 | bytes 6094848 | tf_op jit(solution)/shard_map/ladder_far_pair/pallas_call | solution.py:77
  69.9 0.0 copy-start.5
  69.9 16.0 %all_to_all.15.parts = f32[4,144,384]{2,1,0:T(8,128)S(1)} all-to-all(f32[4,144,384]{2,1,0:T(8,128)S(1)} %ladder_far_pair.1), channel_id=1, replica_groups={{0,4,8,12},{16,20,24,28},{32,36,40,44},{48,52,56,60},{1,5,9,13},{17,21,..., dimensions={0} | all-to-all | bytes 1769472 | tf_op jit(solution)/shard_map/all_to_all | solution.py:201
  85.8 1.3 %add_ladder.1 = f32[144,1536]{1,0:T(8,128)} custom-call(f32[144,1536]{1,0:T(8,128)S(1)} %copy-done.5, f32[4,144,384]{2,1,0:T(8,128)S(1)} %all_to_all.15.parts), custom_call_target="tpu_custom_call" | custom-call | tf_op jit(solution)/shard_map/add_ladder/pallas_call | solution.py:167
  (9 shorter events, 0.0 us)
Async XLA Ops:
  0.0 25.7 %collective-permute-start.2 = (f32[96,2048]{1,0:T(8,128)}, f32[96,2048]{1,0:T(8,128)S(1)}, u32[]{:S(2)}, u32[]{:S(2)}) collective-permute-start(f32[96,2048]{1,0:T(8,128)} %bitcast.1), channel_id=1, source_target_pairs={{0,16},{1,17},{64,80},{65,81},{128,144},{129,145},{192,208},{193,2... | collective-permute-start | bytes 2359304 | tf_op jit(solution)/shard_map/ppermute | solution.py:182
  3.9 21.7 %collective-permute-start.3 = (f32[96,2048]{1,0:T(8,128)}, f32[96,2048]{1,0:T(8,128)S(1)}, u32[]{:S(2)}, u32[]{:S(2)}) collective-permute-start(f32[96,2048]{1,0:T(8,128)} %bitcast.2), channel_id=1, source_target_pairs={{0,48},{1,49},{64,112},{65,113},{128,176},{129,177},{192,240},{193... | collective-permute-start | bytes 2359304 | tf_op jit(solution)/shard_map/ppermute | solution.py:182
  7.1 1.0 %copy-start.4 = (f32[144,512]{1,0:T(8,128)S(1)}, f32[144,512]{1,0:T(8,128)}, u32[]{:S(2)}) copy-start(f32[144,512]{1,0:T(8,128)} %given.1) | copy-start | bytes 884740
  8.9 24.9 %collective-permute-start = (f32[72,512]{1,0:T(8,128)}, f32[72,512]{1,0:T(8,128)}, u32[]{:S(2)}, u32[]{:S(2)}) collective-permute-start(f32[72,512]{1,0:T(8,128)} %share.1), channel_id=1, source_target_pairs={{0,450},{1,451},{64,386},{65,387},{128,322},{129,323},{192,258},{1... | collective-permute-start | bytes 442376 | tf_op jit(solution)/shard_map/ppermute | solution.py:182
  21.4 4.4 %copy-start = (f32[1,1,1,96,2048]{4,3,2,1,0:T(8,128)S(1)}, f32[1,1,1,96,2048]{4,3,2,1,0:T(8,128)}, u32[]{:S(2)}) copy-start(f32[1,1,1,96,2048]{4,3,2,1,0:T(8,128)} %param.4) | copy-start | bytes 2359300
  21.4 19.2 %all-to-all-start.1 = ((f32[4,144,512]{2,1,0:T(8,128)}), f32[4,144,512]{2,1,0:T(8,128)S(1)}, u32[]{:S(2)}, u32[]{:S(2)}) async-start(f32[4,144,512]{2,1,0:T(8,128)} %spread_near.1), calls=%async_computation.1 | async-start | bytes 2359296 | tf_op jit(solution)/shard_map/all_to_all | solution.py:186
  25.7 24.3 %collective-permute-start.4 = (f32[96,2048]{1,0:T(8,128)S(1)}, f32[96,2048]{1,0:T(8,128)}, u32[]{:S(2)}, u32[]{:S(2)}) collective-permute-start(f32[96,2048]{1,0:T(8,128)S(1)} %bitcast.3), channel_id=1, source_target_pairs={{0,32},{1,33},{64,96},{65,97},{128,160},{129,161},{192,224},{193,2... | collective-permute-start | bytes 2359304 | tf_op jit(solution)/shard_map/ppermute | solution.py:182
  36.3 1.0 %copy-start.3 = (f32[8,72,512]{2,1,0:T(8,128)}, f32[8,72,512]{2,1,0:T(8,128)S(1)}, u32[]{:S(2)}) copy-start(f32[8,72,512]{2,1,0:T(8,128)S(1)} %spread_far.1) | copy-start | bytes 3538948
  40.5 1.0 %copy-start.1 = (f32[4,144,512]{2,1,0:T(8,128)}, f32[4,144,512]{2,1,0:T(8,128)S(1)}, u32[]{:S(2)}) copy-start(f32[4,144,512]{2,1,0:T(8,128)S(1)} %all-to-all-done.1.refs_0_) | copy-start | bytes 3538948
  41.6 16.1 %all-to-all-start = ((f32[8,72,512]{2,1,0:T(8,128)}), f32[8,72,512]{2,1,0:T(8,128)S(1)}, u32[]{:S(2)}, u32[]{:S(2)}) async-start(f32[8,72,512]{2,1,0:T(8,128)} %copy-done.3), calls=%async_computation | async-start | bytes 2359296 | tf_op jit(solution)/shard_map/all_to_all | solution.py:190
  45.1 7.5 %copy-start.2 = (f32[4,144,512]{2,1,0:T(8,128)S(1)}, f32[4,144,512]{2,1,0:T(8,128)}, u32[]{:S(2)}) copy-start(f32[4,144,512]{2,1,0:T(8,128)} %copy-done.1) | copy-start | bytes 3538948
  45.2 7.5 %collective-permute-start.1 = (f32[4,144,512]{2,1,0:T(8,128)}, f32[4,144,512]{2,1,0:T(8,128)S(1)}, u32[]{:S(2)}, u32[]{:S(2)}) collective-permute-start(f32[4,144,512]{2,1,0:T(8,128)} %copy-done.1), channel_id=1, source_target_pairs={{0,1},{1,0},{64,65},{65,64},{128,129},{129,128},{192,193},{193,192... | collective-permute-start | bytes 3538952 | tf_op jit(solution)/shard_map/ppermute | solution.py:182
  55.9 0.9 %copy-start.6 = (f32[4,144,384]{2,1,0:T(8,128)}, f32[4,144,384]{2,1,0:T(8,128)S(1)}, u32[]{:S(2)}) copy-start(f32[4,144,384]{2,1,0:T(8,128)S(1)} %ladder_near.1.refs_0_) | copy-start | bytes 2654212
  57.6 9.9 %collective-permute-start.5 = (f32[8,72,512]{2,1,0:T(8,128)S(1)}, f32[8,72,512]{2,1,0:T(8,128)S(1)}, u32[]{:S(2)}, u32[]{:S(2)}) collective-permute-start(f32[8,72,512]{2,1,0:T(8,128)S(1)} %all-to-all-done.refs_1_), channel_id=1, source_target_pairs={{0,1},{1,0},{64,65},{65,64},{128,129},{129,128},{192,193},{193,192... | collective-permute-start | bytes 3538952 | tf_op jit(solution)/shard_map/ppermute | solution.py:182
  64.1 1.2 %copy-start.7 = (f32[4,144,384]{2,1,0:T(8,128)S(1)}, f32[4,144,384]{2,1,0:T(8,128)}, u32[]{:S(2)}) copy-start(f32[4,144,384]{2,1,0:T(8,128)} %copy-done.6) | copy-start | bytes 2654212
  69.9 16.0 %copy-start.5 = (f32[144,1536]{1,0:T(8,128)S(1)}, f32[144,1536]{1,0:T(8,128)}, u32[]{:S(2)}) copy-start(f32[144,1536]{1,0:T(8,128)} %residual.1) | copy-start | bytes 2654212

commit v3 on v2

--- a/solution.py
+++ b/solution.py
@@ -10,8 +10,10 @@
 AXES = ("row", "col", "layer")
 SIDE = 4
 LIMIT = 24 * 2**20
+ALL = 67043328
 FAKE = 12 * 10**9
 PRICE = 20.0
+FETCH = True
 GATE = 10 * 10**9
 
 
@@ -53,41 +55,85 @@
     return one(a_high, b_high) + (one(a_high, b_low) + one(a_low, b_high))
 
 
-def ladder_kernel(turns, accumulate, n_blocks, *refs):
+def ladder_kernel(turns, accumulate, fetch, n_blocks, *refs):
+    n = len(turns)
     if accumulate:
         so_far, refs = refs[0], refs[1:]
-    terms, blocks, out = refs[: len(turns)], refs[len(turns) : len(turns) + n_blocks], refs[-1]
+    terms, blocks, refs = refs[:n], refs[n : n + n_blocks], refs[n + n_blocks :]
+    own = 3 + accumulate * 2 + fetch * 2
+    out, v_ref, v_sems, *rest = refs[-own:]
     layer = lax.axis_index("layer")
-    ys, rows, _ = out.shape
+    width = v_ref.shape[2]
+    waits = []
+    for k, (far, swapped) in enumerate(turns):
+        at_layer = ((layer // 2) ^ far) * 2 + ((layer % 2) ^ swapped)
+        at = pl.ds(pl.multiple_of(at_layer * width, width), width)
+        copies = []
+        if fetch:
+            copies.append(pltpu.make_async_copy(terms[k], rest[-2].at[k], rest[-1].at[k]))
+        row = 0
+        for m, block in enumerate(blocks):
+            taken = v_ref.at[k, pl.ds(row, block.shape[0])]
+            copies.append(pltpu.make_async_copy(block.at[:, at], taken, v_sems.at[k, m]))
+            row += block.shape[0]
+        waits.append(copies)
+    if accumulate:
+        waits.append([pltpu.make_async_copy(so_far, rest[0], rest[1])])
+    for copies in waits:
+        for copy in copies:
+            copy.start()
     total = None
-    for (far, swapped), t_ref in zip(turns, terms, strict=True):
-        at_layer = ((layer // 2) ^ far) * 2 + ((layer % 2) ^ swapped)
-        pieces, _, width = t_ref.shape
-        at = pl.ds(pl.multiple_of(at_layer * width, width), width)
-        v = jnp.concatenate([b[:, at] for b in blocks], axis=0)
-        t = jnp.concatenate([t_ref[part * ys + y] for y in range(ys) for part in range(pieces // ys)], axis=0)
-        total = times(t, v) if total is None else total + times(t, v)
+    for k in range(n):
+        if fetch:
+            for copy in waits[k]:
+                copy.wait()
+        t_ref = rest[-2].at[k] if fetch else terms[k]
+        pieces = t_ref.shape[0] // SIDE
+        t = jnp.concatenate([t_ref[part * SIDE + y] for y in range(SIDE) for part in range(pieces)], axis=0)
+        if not fetch:
+            for copy in waits[k]:
+                copy.wait()
+        term = times(t, v_ref[k])
+        total = term if total is None else total + term
     total = total.reshape(out.shape)
-    out[...] = so_far[...] + total if accumulate else total
-
-
-def ladder(turns, so_far, terms, blocks, shape, name, price=1.0, after=()):
-    given = (() if so_far is None else (so_far,)) + (*terms, *blocks)
-    flops = 2 * 3 * shape[0] * shape[1] * shape[2] * len(turns) * terms[0].shape[-1]
-    return pl.pallas_call(
-        functools.partial(ladder_kernel, turns, so_far is not None, len(blocks)),
+    if accumulate:
+        waits[n][0].wait()
+        total = rest[0][...] + total
+    out[...] = total
+
+
+def ladder(turns, so_far, terms, blocks, shape, name, price=1.0, after=(), fetch=False):
+    width, columns = terms[0].shape[-1], shape[-1]
+    given = (() if so_far is None else (so_far,)) + (*terms, *blocks, *after)
+    flops = 2 * 3 * shape[0] * shape[1] * columns * len(turns) * width
+    here, there = pl.BlockSpec(memory_space=pltpu.VMEM), pl.BlockSpec(memory_space=pl.ANY)
+    scratch = [
+        pltpu.VMEM((len(turns), columns, width), jnp.float32),
+        pltpu.SemaphoreType.DMA((len(turns), len(blocks))),
+    ]
+    if so_far is not None:
+        scratch += [pltpu.VMEM(shape, jnp.float32), pltpu.SemaphoreType.DMA]
+    if fetch:
+        scratch += [
+            pltpu.VMEM((len(turns), *terms[0].shape), jnp.float32),
+            pltpu.SemaphoreType.DMA((len(turns),)),
+        ]
+    return pl.pallas_call(
+        functools.partial(ladder_kernel, turns, so_far is not None, fetch, len(blocks)),
         out_shape=jax.ShapeDtypeStruct(shape, jnp.float32),
-        in_specs=[pl.BlockSpec(memory_space=pltpu.VMEM)] * len(given)
-        + [pl.BlockSpec(memory_space=pl.ANY)] * len(after),
-        out_specs=pl.BlockSpec(memory_space=pltpu.VMEM),
+        in_specs=[there] * (so_far is not None)
+        + [there if fetch else here] * len(terms)
+        + [there] * (len(blocks) + len(after)),
+        out_specs=here,
+        scratch_shapes=scratch,
         cost_estimate=pl.CostEstimate(
             flops=int(flops * price),
-            bytes_accessed=4 * sum(a.size for a in given) + 4 * shape[0] * shape[1] * shape[2],
+            bytes_accessed=4 * (len(turns) * (terms[0].size + columns * width)),
             transcendentals=0,
         ),
         compiler_params=pltpu.CompilerParams(vmem_limit_bytes=LIMIT),
         name=name,
-    )(*given, *after)
+    )(*given)
 
 
 def gate_kernel(*refs):
@@ -106,8 +152,11 @@
     )(*values)
 
 
-def spread_kernel(given, whole, sems):
-    copies = [pltpu.make_async_copy(given, whole.at[k], sems.at[k]) for k in range(whole.shape[0])]
+def spread_kernel(given, whole, held, sem, sems):
+    fetched = pltpu.make_async_copy(given, held, sem)
+    fetched.start()
+    fetched.wait()
+    copies = [pltpu.make_async_copy(held, whole.at[k], sems.at[k]) for k in range(whole.shape[0])]
     for copy in copies:
         copy.start()
     for copy in copies:
@@ -118,13 +167,17 @@
     return pl.pallas_call(
         spread_kernel,
         out_shape=jax.ShapeDtypeStruct((copies, *value.shape), jnp.float32),
-        in_specs=[pl.BlockSpec(memory_space=pltpu.VMEM)],
+        in_specs=[pl.BlockSpec(memory_space=pl.ANY)],
         out_specs=pl.BlockSpec(memory_space=pltpu.HBM),
-        scratch_shapes=[pltpu.SemaphoreType.DMA((copies,))],
+        scratch_shapes=[
+            pltpu.VMEM(value.shape, jnp.float32),
+            pltpu.SemaphoreType.DMA,
+            pltpu.SemaphoreType.DMA((copies,)),
+        ],
         cost_estimate=pl.CostEstimate(
             flops=price, bytes_accessed=4 * value.size * (1 + copies), transcendentals=0
         ),
-        compiler_params=pltpu.CompilerParams(vmem_limit_bytes=LIMIT),
+        compiler_params=pltpu.CompilerParams(vmem_limit_bytes=ALL),
         name=name,
     )(value)
 
@@ -193,7 +246,7 @@
     blocks = (v, v_left, v_right, v_across)
     shape = (SIDE, rows, SIDE * v.shape[0])
     arrived = (gate((v_across,), GATE),)
-    total = ladder(((0, 0), (0, 1)), None, (near, near_pair), blocks, shape, "ladder_near", PRICE, arrived)
+    total = ladder(((0, 0), (0, 1)), None, (near, near_pair), blocks, shape, "ladder_near", PRICE, arrived, FETCH)
     far, total = lax.optimization_barrier((far, total))
     far_pair = send(far, swap=True)
     total = ladder(((1, 0),), total, (far,), blocks, shape, "ladder_far")

time: 87.8 us -> 86.5 us (0.985)
  local copies, waits for them, and re-layouts: 5.09 us -> 0.96 us
  waiting for transfers between devices: 11.4 us -> 13.3 us
  Pallas kernels: 13.4 us -> 14.8 us
    unnamed x16 -> x4, local copies, waits for them, and re-layouts: 5.09 us -> 0.96 us
    all_to_all x1, waiting for transfers between devices: 3.17 us -> 5.54 us  [on_device(): lax.all_to_all(spread(t, SIDE, 'spread_near'), 'col', 0, 0, axis_index_gr...]
    pallas_call x3, Pallas kernels: 7.67 us -> 8.61 us  [ladder(): pl.pallas_call(functools.partial(ladder_kernel, turns, so_far is not None...]
    ppermute x6, waiting for transfers between devices: 7.35 us -> 6.45 us  [send(): return lax.ppermute(value, AXES, shifted(**move))]
  transfers between devices with their start and end apart: 8 -> 8, of which waited for: 4 -> 4; matrix products, arithmetic and copies ran while one was open for 0% -> 0% of each run, Pallas kernels for 11% -> 13%
where the time goes in v3:
time: 86.5 us; the launch traced here: 85.7 us
  starting transfers between devices  41.1 us (48%)
  blocking collectives  15.4 us (18%)
  Pallas kernels  14.8 us (17%)
  waiting for transfers between devices  13.3 us (15%)
  local copies, waits for them, and re-layouts  0.96 us (1%)
    ppermute x6, starting transfers between devices, send(): return lax.ppermute(value, AXES, shifted(**move))  33.2 us
    all_to_all x1, blocking collectives, on_device(): parts = lax.all_to_all(total, 'col', 0, 0, axis_index_groups=Y_RINGS)  15.4 us
    pallas_call x3, Pallas kernels, ladder(): pl.pallas_call(functools.partial(ladder_kernel, turns, so_far is not None...  8.61 us
    ppermute x6, waiting for transfers between devices, send(): return lax.ppermute(value, AXES, shifted(**move))  6.45 us
    all_to_all x1, waiting for transfers between devices, on_device(): lax.all_to_all(spread(t, SIDE, 'spread_near'), 'col', 0, 0, axis_index_gr...  5.54 us
    all_to_all x1, starting transfers between devices, on_device(): lax.all_to_all(spread(t, SIDE, 'spread_near'), 'col', 0, 0, axis_index_gr...  4.27 us
    pallas_call x2, Pallas kernels, spread(): pl.pallas_call(spread_kernel, out_shape=jax.ShapeDtypeStruct((copies, *va...  4.05 us
    all_to_all x1, starting transfers between devices, on_device(): lax.all_to_all(far, ('row', 'col'), 0, 0, axis_index_groups=Y_RINGS_OF_TWO)  3.56 us
  transfers between devices with their start and end apart: 8, of which 4 were waited for; matrix products, arithmetic and copies ran while one was open for 0% of the time, Pallas kernels for 13%

profile of v3, /device:TPU:1, one launch (start us, length us, event | category | flops | bytes accessed | tf_op | source)
XLA Modules:
  0.0 85.7 jit_solution(2903810140695485987)
XLA Ops:
  0.0 3.9 %collective-permute-start.2 = (f32[96,2048]{1,0:T(8,128)}, f32[96,2048]{1,0:T(8,128)}, u32[]{:S(2)}, u32[]{:S(2)}) collective-permute-start(f32[96,2048]{1,0:T(8,128)} %bitcast.refs_2_), channel_id=1, source_target_pairs={{0,16},{1,17},{64,80},{65,81},{128,144},{129,145},{192,208},{193,2... | collective-permute-start | bytes 2359304 | tf_op jit(solution)/shard_map/ppermute | solution.py:235
  3.9 3.2 %collective-permute-start.3 = (f32[96,2048]{1,0:T(8,128)}, f32[96,2048]{1,0:T(8,128)}, u32[]{:S(2)}, u32[]{:S(2)}) collective-permute-start(f32[96,2048]{1,0:T(8,128)} %bitcast.refs_2_), channel_id=1, source_target_pairs={{0,48},{1,49},{64,112},{65,113},{128,176},{129,177},{192,240},{193... | collective-permute-start | bytes 2359304 | tf_op jit(solution)/shard_map/ppermute | solution.py:235
  7.1 0.0 copy-start
  7.2 1.0 %copy-done = f32[144,512]{1,0:T(8,128)S(1)} copy-done((f32[144,512]{1,0:T(8,128)S(1)}, f32[144,512]{1,0:T(8,128)}, u32[]{:S(2)}) %copy-start) | copy-done | bytes 294936
  8.1 0.8 share.1
  8.9 11.3 %collective-permute-start = (f32[72,512]{1,0:T(8,128)}, f32[72,512]{1,0:T(8,128)}, u32[]{:S(2)}, u32[]{:S(2)}) collective-permute-start(f32[72,512]{1,0:T(8,128)} %share.1), channel_id=1, source_target_pairs={{0,450},{1,451},{64,386},{65,387},{128,322},{129,323},{192,258},{1... | collective-permute-start | bytes 442376 | tf_op jit(solution)/shard_map/ppermute | solution.py:235
  20.3 2.0 %spread_near.1 = f32[4,144,512]{2,1,0:T(8,128)} custom-call(f32[144,512]{1,0:T(8,128)} %given.1), custom_call_target="tpu_custom_call" | custom-call | bytes 1474560 | tf_op jit(solution)/shard_map/spread_near/pallas_call | solution.py:167
  22.3 4.3 %all-to-all-start.1 = ((f32[4,144,512]{2,1,0:T(8,128)}), f32[4,144,512]{2,1,0:T(8,128)}, u32[]{:S(2)}, u32[]{:S(2)}) async-start(f32[4,144,512]{2,1,0:T(8,128)} %spread_near.1), calls=%async_computation.1 | async-start | bytes 2359296 | tf_op jit(solution)/shard_map/all_to_all | solution.py:239
  26.6 0.0 collective-permute-done.2.refs_3_
  26.6 0.0 collective-permute-done.3.refs_4_
  26.6 3.4 %collective-permute-start.4 = (f32[96,2048]{1,0:T(8,128)}, f32[96,2048]{1,0:T(8,128)}, u32[]{:S(2)}, u32[]{:S(2)}) collective-permute-start(f32[96,2048]{1,0:T(8,128)} %bitcast.refs_2_), channel_id=1, source_target_pairs={{0,32},{1,33},{64,96},{65,97},{128,160},{129,161},{192,224},{193,2... | collective-permute-start | bytes 2359304 | tf_op jit(solution)/shard_map/ppermute | solution.py:235
  30.1 3.8 %collective-permute-done.given = f32[72,512]{1,0:T(8,128)} collective-permute-done((f32[72,512]{1,0:T(8,128)}, f32[72,512]{1,0:T(8,128)}, u32[]{:S(2)}, u32[]{:S(2)}) %collective-permute-start) | collective-permute-done | bytes 147488 | tf_op jit(solution)/shard_map/ppermute | solution.py:235
  33.9 2.0 %spread_far.1 = f32[8,72,512]{2,1,0:T(8,128)} custom-call(f32[72,512]{1,0:T(8,128)} %collective-permute-done.given), custom_call_target="tpu_custom_call" | custom-call | flops 12000000000 | bytes 1327104 | tf_op jit(solution)/shard_map/spread_far/pallas_call | solution.py:167
  35.9 5.5 %all-to-all-done.1.refs_0_ = f32[4,144,512]{2,1,0:T(8,128)} async-done(((f32[4,144,512]{2,1,0:T(8,128)}), f32[4,144,512]{2,1,0:T(8,128)}, u32[]{:S(2)}, u32[]{:S(2)}) %all-to-all-start.1) | async-done | bytes 1179680 | tf_op jit(solution)/shard_map/all_to_all | solution.py:239
  41.4 3.6 %all-to-all-start = ((f32[8,72,512]{2,1,0:T(8,128)}), f32[8,72,512]{2,1,0:T(8,128)S(1)}, u32[]{:S(2)}, u32[]{:S(2)}) async-start(f32[8,72,512]{2,1,0:T(8,128)} %spread_far.1), calls=%async_computation | async-start | bytes 2359296 | tf_op jit(solution)/shard_map/all_to_all | solution.py:243
  45.0 4.8 %collective-permute-start.1 = (f32[4,144,512]{2,1,0:T(8,128)}, f32[4,144,512]{2,1,0:T(8,128)S(1)}, u32[]{:S(2)}, u32[]{:S(2)}) collective-permute-start(f32[4,144,512]{2,1,0:T(8,128)} %all-to-all-done.1.refs_0_), channel_id=1, source_target_pairs={{0,1},{1,0},{64,65},{65,64},{128,129},{129,128},{192,193},{193,192... | collective-permute-start | bytes 3538952 | tf_op jit(solution)/shard_map/ppermute | solution.py:235
  49.8 0.0 collective-permute-done.4.refs_0_.refs_5_
  49.8 2.6 %collective-permute-done.1.refs_1_ = f32[4,144,512]{2,1,0:T(8,128)S(1)} collective-permute-done((f32[4,144,512]{2,1,0:T(8,128)}, f32[4,144,512]{2,1,0:T(8,128)S(1)}, u32[]{:S(2)}, u32[]{:S(2)}) %collective-permute-start.1) | collective-permute-done | bytes 1179680 | tf_op jit(solution)/shard_map/ppermute | solution.py:235
  52.5 3.7 %ladder_near.1.refs_0_ = f32[4,144,384]{2,1,0:T(8,128)S(1)} custom-call(f32[4,144,512]{2,1,0:T(8,128)} %all-to-all-done.1.refs_0_, f32[4,144,512]{2,1,0:T(8,128)S(1)} %collective-permute-done.1.refs_1_, f32[96,2048]{1,0:T(8,128)} %bitcast.refs_2_, f32[96,2048]{1,0:T(8,128)} %collective-permute-done.2.refs_3_, f32[96,2048]{1,0:T(8,128)} %collective-permute-done.3.refs_4_, ...), custom_call_target="tpu_custom_call" | custom-call | flops 27179089920 | bytes 3932160 | tf_op jit(solution)/shard_map/ladder_near/pallas_call | solution.py:121
  56.1 1.3 %all-to-all-done.refs_1_ = f32[8,72,512]{2,1,0:T(8,128)S(1)} async-done(((f32[8,72,512]{2,1,0:T(8,128)}), f32[8,72,512]{2,1,0:T(8,128)S(1)}, u32[]{:S(2)}, u32[]{:S(2)}) %all-to-all-start) | async-done | bytes 1179680 | tf_op jit(solution)/shard_map/all_to_all | solution.py:243
  57.4 6.6 %collective-permute-start.5 = (f32[8,72,512]{2,1,0:T(8,128)S(1)}, f32[8,72,512]{2,1,0:T(8,128)S(1)}, u32[]{:S(2)}, u32[]{:S(2)}) collective-permute-start(f32[8,72,512]{2,1,0:T(8,128)S(1)} %all-to-all-done.refs_1_), channel_id=1, source_target_pairs={{0,1},{1,0},{64,65},{65,64},{128,129},{129,128},{192,193},{193,192... | collective-permute-start | bytes 3538952 | tf_op jit(solution)/shard_map/ppermute | solution.py:235
  64.0 2.5 %ladder_far.1.refs_0_ = f32[4,144,384]{2,1,0:T(8,128)S(1)} custom-call(f32[4,144,384]{2,1,0:T(8,128)S(1)} %ladder_near.1.refs_0_, f32[8,72,512]{2,1,0:T(8,128)S(1)} %all-to-all-done.refs_1_, f32[96,2048]{1,0:T(8,128)} %bitcast.refs_2_, f32[96,2048]{1,0:T(8,128)} %collective-permute-done.2.refs_3_, f32[96,2048]{1,0:T(8,128)} %collective-permute-done.3.refs_4_, ...), custom_call_target="tpu_custom_call" | custom-call | flops 679477248 | bytes 1966080 | tf_op jit(solution)/shard_map/ladder_far/pallas_call | solution.py:121
  66.5 0.0 collective-permute-done.5.refs_1_
  66.5 2.5 %ladder_far_pair.1 = f32[4,144,384]{2,1,0:T(8,128)S(1)} custom-call(f32[4,144,384]{2,1,0:T(8,128)S(1)} %ladder_far.1.refs_0_, f32[8,72,512]{2,1,0:T(8,128)S(1)} %collective-permute-done.5.refs_1_, f32[96,2048]{1,0:T(8,128)} %bitcast.refs_2_, f32[96,2048]{1,0:T(8,128)} %collective-permute-done.2.refs_3_, f32[96,2048]{1,0:T(8,128)} %collective-permute-done.3.refs_4_, ...), custom_call_target="tpu_custom_call" | custom-call | flops 679477248 | bytes 1966080 | tf_op jit(solution)/shard_map/ladder_far_pair/pallas_call | solution.py:121
  69.0 0.0 copy-start.1
  69.0 15.4 %all_to_all.15.parts = f32[4,144,384]{2,1,0:T(8,128)S(1)} all-to-all(f32[4,144,384]{2,1,0:T(8,128)S(1)} %ladder_far_pair.1), channel_id=1, replica_groups={{0,4,8,12},{16,20,24,28},{32,36,40,44},{48,52,56,60},{1,5,9,13},{17,21,..., dimensions={0} | all-to-all | bytes 1769472 | tf_op jit(solution)/shard_map/all_to_all | solution.py:254
  84.3 0.0 copy-done.1
  84.3 1.3 %add_ladder.1 = f32[144,1536]{1,0:T(8,128)} custom-call(f32[144,1536]{1,0:T(8,128)S(1)} %copy-done.1, f32[4,144,384]{2,1,0:T(8,128)S(1)} %all_to_all.15.parts), custom_call_target="tpu_custom_call" | custom-call | tf_op jit(solution)/shard_map/add_ladder/pallas_call | solution.py:220
  (1 shorter events, 0.0 us)
Async XLA Ops:
  0.0 26.6 %collective-permute-start.2 = (f32[96,2048]{1,0:T(8,128)}, f32[96,2048]{1,0:T(8,128)}, u32[]{:S(2)}, u32[]{:S(2)}) collective-permute-start(f32[96,2048]{1,0:T(8,128)} %bitcast.refs_2_), channel_id=1, source_target_pairs={{0,16},{1,17},{64,80},{65,81},{128,144},{129,145},{192,208},{193,2... | collective-permute-start | bytes 2359304 | tf_op jit(solution)/shard_map/ppermute | solution.py:235
  3.9 22.7 %collective-permute-start.3 = (f32[96,2048]{1,0:T(8,128)}, f32[96,2048]{1,0:T(8,128)}, u32[]{:S(2)}, u32[]{:S(2)}) collective-permute-start(f32[96,2048]{1,0:T(8,128)} %bitcast.refs_2_), channel_id=1, source_target_pairs={{0,48},{1,49},{64,112},{65,113},{128,176},{129,177},{192,240},{193... | collective-permute-start | bytes 2359304 | tf_op jit(solution)/shard_map/ppermute | solution.py:235
  7.1 1.0 %copy-start = (f32[144,512]{1,0:T(8,128)S(1)}, f32[144,512]{1,0:T(8,128)}, u32[]{:S(2)}) copy-start(f32[144,512]{1,0:T(8,128)} %given.1) | copy-start | bytes 884740
  8.9 24.9 %collective-permute-start = (f32[72,512]{1,0:T(8,128)}, f32[72,512]{1,0:T(8,128)}, u32[]{:S(2)}, u32[]{:S(2)}) collective-permute-start(f32[72,512]{1,0:T(8,128)} %share.1), channel_id=1, source_target_pairs={{0,450},{1,451},{64,386},{65,387},{128,322},{129,323},{192,258},{1... | collective-permute-start | bytes 442376 | tf_op jit(solution)/shard_map/ppermute | solution.py:235
  22.3 19.1 %all-to-all-start.1 = ((f32[4,144,512]{2,1,0:T(8,128)}), f32[4,144,512]{2,1,0:T(8,128)}, u32[]{:S(2)}, u32[]{:S(2)}) async-start(f32[4,144,512]{2,1,0:T(8,128)} %spread_near.1), calls=%async_computation.1 | async-start | bytes 2359296 | tf_op jit(solution)/shard_map/all_to_all | solution.py:239
  26.6 23.2 %collective-permute-start.4 = (f32[96,2048]{1,0:T(8,128)}, f32[96,2048]{1,0:T(8,128)}, u32[]{:S(2)}, u32[]{:S(2)}) collective-permute-start(f32[96,2048]{1,0:T(8,128)} %bitcast.refs_2_), channel_id=1, source_target_pairs={{0,32},{1,33},{64,96},{65,97},{128,160},{129,161},{192,224},{193,2... | collective-permute-start | bytes 2359304 | tf_op jit(solution)/shard_map/ppermute | solution.py:235
  41.4 16.0 %all-to-all-start = ((f32[8,72,512]{2,1,0:T(8,128)}), f32[8,72,512]{2,1,0:T(8,128)S(1)}, u32[]{:S(2)}, u32[]{:S(2)}) async-start(f32[8,72,512]{2,1,0:T(8,128)} %spread_far.1), calls=%async_computation | async-start | bytes 2359296 | tf_op jit(solution)/shard_map/all_to_all | solution.py:243
  45.0 7.5 %collective-permute-start.1 = (f32[4,144,512]{2,1,0:T(8,128)}, f32[4,144,512]{2,1,0:T(8,128)S(1)}, u32[]{:S(2)}, u32[]{:S(2)}) collective-permute-start(f32[4,144,512]{2,1,0:T(8,128)} %all-to-all-done.1.refs_0_), channel_id=1, source_target_pairs={{0,1},{1,0},{64,65},{65,64},{128,129},{129,128},{192,193},{193,192... | collective-permute-start | bytes 3538952 | tf_op jit(solution)/shard_map/ppermute | solution.py:235
  57.4 9.0 %collective-permute-start.5 = (f32[8,72,512]{2,1,0:T(8,128)S(1)}, f32[8,72,512]{2,1,0:T(8,128)S(1)}, u32[]{:S(2)}, u32[]{:S(2)}) collective-permute-start(f32[8,72,512]{2,1,0:T(8,128)S(1)} %all-to-all-done.refs_1_), channel_id=1, source_target_pairs={{0,1},{1,0},{64,65},{65,64},{128,129},{129,128},{192,193},{193,192... | collective-permute-start | bytes 3538952 | tf_op jit(solution)/shard_map/ppermute | solution.py:235
  69.0 15.4 %copy-start.1 = (f32[144,1536]{1,0:T(8,128)S(1)}, f32[144,1536]{1,0:T(8,128)}, u32[]{:S(2)}) copy-start(f32[144,1536]{1,0:T(8,128)} %residual.1) | copy-start | bytes 2654212

commit v4 on v3

--- a/solution.py
+++ b/solution.py
@@ -152,15 +152,25 @@
     )(*values)
 
 
-def spread_kernel(given, whole, held, sem, sems):
-    fetched = pltpu.make_async_copy(given, held, sem)
-    fetched.start()
-    fetched.wait()
-    copies = [pltpu.make_async_copy(held, whole.at[k], sems.at[k]) for k in range(whole.shape[0])]
-    for copy in copies:
-        copy.start()
-    for copy in copies:
-        copy.wait()
+def spread_kernel(given, whole, held, fetch_sems, sems):
+    chunks = fetch_sems.shape[0]
+    rows = given.shape[0] // chunks
+    fetches, copies = [], []
+    for c in range(chunks):
+        at = pl.ds(c * rows, rows)
+        fetches.append(pltpu.make_async_copy(given.at[at], held.at[at], fetch_sems.at[c]))
+        copies.append(
+            [pltpu.make_async_copy(held.at[at], whole.at[k, at], sems.at[c, k]) for k in range(whole.shape[0])]
+        )
+    for fetch in fetches:
+        fetch.start()
+    for fetch, sends in zip(fetches, copies, strict=True):
+        fetch.wait()
+        for copy in sends:
+            copy.start()
+    for sends in copies:
+        for copy in sends:
+            copy.wait()
 
 
 def spread(value, copies, name, price=0):
@@ -171,8 +181,8 @@
         out_specs=pl.BlockSpec(memory_space=pltpu.HBM),
         scratch_shapes=[
             pltpu.VMEM(value.shape, jnp.float32),
-            pltpu.SemaphoreType.DMA,
-            pltpu.SemaphoreType.DMA((copies,)),
+            pltpu.SemaphoreType.DMA((3,)),
+            pltpu.SemaphoreType.DMA((3, copies)),
         ],
         cost_estimate=pl.CostEstimate(
             flops=price, bytes_accessed=4 * value.size * (1 + copies), transcendentals=0
@@ -180,28 +190,6 @@
         compiler_params=pltpu.CompilerParams(vmem_limit_bytes=ALL),
         name=name,
     )(value)
-
-
-def share_kernel(t, out, sem):
-    rows = out.shape[0]
-    at = pl.ds(pl.multiple_of((1 - lax.axis_index("row") % 2) * rows, 8), rows)
-    copy = pltpu.make_async_copy(t.at[at], out, sem)
-    copy.start()
-    copy.wait()
-
-
-def share_of(t):
-    rows, width = t.shape
-    return pl.pallas_call(
-        share_kernel,
-        out_shape=jax.ShapeDtypeStruct((rows // 2, width), jnp.float32),
-        in_specs=[pl.BlockSpec(memory_space=pl.ANY)],
-        out_specs=pl.BlockSpec(memory_space=pltpu.VMEM),
-        scratch_shapes=[pltpu.SemaphoreType.DMA],
-        cost_estimate=pl.CostEstimate(flops=0, bytes_accessed=4 * t.size, transcendentals=0),
-        compiler_params=pltpu.CompilerParams(vmem_limit_bytes=LIMIT),
-        name="share",
-    )(t)
 
 
 def add_kernel(order, residual, parts, out):
@@ -234,7 +222,9 @@
     def send(value, **move):
         return lax.ppermute(value, AXES, shifted(**move))
 
-    share_far = send(share_of(t), mirror=True)
+    half = rows // 2
+    share = lax.dynamic_slice_in_dim(t, (1 - lax.axis_index("row") % 2) * half, half, 0)
+    share_far = send(share, mirror=True)
     v_left, v_right = send(v, dx=1), send(v, dx=-1)
     near = lax.all_to_all(spread(t, SIDE, "spread_near"), "col", 0, 0, axis_index_groups=Y_RINGS)
     v_left, v_right, v_next = lax.optimization_barrier((v_left, v_right, v))

time: 86.5 us -> 86.3 us (level)
    dynamic_slice x0 -> x1, local copies, waits for them, and re-layouts: none -> 1.59 us  [on_device(): lax.dynamic_slice_in_dim(t, (1 - lax.axis_index('row') % 2) * half, half, 0)]
    unnamed x4 -> x2, local copies, waits for them, and re-layouts: 0.96 us -> 0.01 us
  transfers between devices with their start and end apart: 8 -> 8, of which waited for: 4 -> 4; matrix products, arithmetic and copies ran while one was open for 0% -> 2% of each run, Pallas kernels for 13% -> 12%
where the time goes in v4:
time: 86.3 us; the launch traced here: 85.5 us
  starting transfers between devices  41 us (48%)
  blocking collectives  15.4 us (18%)
  Pallas kernels  14.1 us (16%)
  waiting for transfers between devices  13.3 us (15%)
  local copies, waits for them, and re-layouts  1.59 us (2%)
    ppermute x6, starting transfers between devices, send(): return lax.ppermute(value, AXES, shifted(**move))  33.2 us
    all_to_all x1, blocking collectives, on_device(): parts = lax.all_to_all(total, 'col', 0, 0, axis_index_groups=Y_RINGS)  15.4 us
    pallas_call x3, Pallas kernels, ladder(): pl.pallas_call(functools.partial(ladder_kernel, turns, so_far is not None...  8.61 us
    ppermute x6, waiting for transfers between devices, send(): return lax.ppermute(value, AXES, shifted(**move))  6.41 us
    all_to_all x1, waiting for transfers between devices, on_device(): lax.all_to_all(spread(t, SIDE, 'spread_near'), 'col', 0, 0, axis_index_gr...  5.54 us
    all_to_all x1, starting transfers between devices, on_device(): lax.all_to_all(spread(t, SIDE, 'spread_near'), 'col', 0, 0, axis_index_gr...  4.28 us
    pallas_call x2, Pallas kernels, spread(): pl.pallas_call(spread_kernel, out_shape=jax.ShapeDtypeStruct((copies, *va...  4.12 us
    all_to_all x1, starting transfers between devices, on_device(): lax.all_to_all(far, ('row', 'col'), 0, 0, axis_index_groups=Y_RINGS_OF_TWO)  3.56 us
  transfers between devices with their start and end apart: 8, of which 4 were waited for; matrix products, arithmetic and copies ran while one was open for 2% of the time, Pallas kernels for 12%

profile of v4, /device:TPU:1, one launch (start us, length us, event | category | flops | bytes accessed | tf_op | source)
XLA Modules:
  0.0 85.5 jit_solution(16469224594145008041)
XLA Ops:
  0.0 3.9 %collective-permute-start.2 = (f32[96,2048]{1,0:T(8,128)}, f32[96,2048]{1,0:T(8,128)}, u32[]{:S(2)}, u32[]{:S(2)}) collective-permute-start(f32[96,2048]{1,0:T(8,128)} %bitcast.refs_2_), channel_id=1, source_target_pairs={{0,16},{1,17},{64,80},{65,81},{128,144},{129,145},{192,208},{193,2... | collective-permute-start | bytes 2359304 | tf_op jit(solution)/shard_map/ppermute | solution.py:223
  3.9 3.2 %collective-permute-start.3 = (f32[96,2048]{1,0:T(8,128)}, f32[96,2048]{1,0:T(8,128)}, u32[]{:S(2)}, u32[]{:S(2)}) collective-permute-start(f32[96,2048]{1,0:T(8,128)} %bitcast.refs_2_), channel_id=1, source_target_pairs={{0,48},{1,49},{64,112},{65,113},{128,176},{129,177},{192,240},{193... | collective-permute-start | bytes 2359304 | tf_op jit(solution)/shard_map/ppermute | solution.py:223
  7.2 1.6 %constant_dynamic-slice_fusion = f32[72,512]{1,0:T(8,128)} fusion(f32[144,512]{1,0:T(8,128)} %given.1, s32[]{:T(128)S(6)} %select_n.11), kind=kLoop, calls=%fused_computation | loop fusion | bytes 294916 | tf_op jit(solution)/shard_map/dynamic_slice | solution.py:226
  8.7 11.3 %collective-permute-start = (f32[72,512]{1,0:T(8,128)}, f32[72,512]{1,0:T(8,128)}, u32[]{:S(2)}, u32[]{:S(2)}) collective-permute-start(f32[72,512]{1,0:T(8,128)} %constant_dynamic-slice_fusion), channel_id=1, source_target_pairs={{0,450},{1,451},{64,386},{65,387},{128,322},{129,323},{192,258},{1... | collective-permute-start | bytes 442376 | tf_op jit(solution)/shard_map/ppermute | solution.py:223
  20.1 2.1 %spread_near.1 = f32[4,144,512]{2,1,0:T(8,128)} custom-call(f32[144,512]{1,0:T(8,128)} %given.1), custom_call_target="tpu_custom_call" | custom-call | bytes 1474560 | tf_op jit(solution)/shard_map/spread_near/pallas_call | solution.py:177
  22.1 4.3 %all-to-all-start.1 = ((f32[4,144,512]{2,1,0:T(8,128)}), f32[4,144,512]{2,1,0:T(8,128)}, u32[]{:S(2)}, u32[]{:S(2)}) async-start(f32[4,144,512]{2,1,0:T(8,128)} %spread_near.1), calls=%async_computation.1 | async-start | bytes 2359296 | tf_op jit(solution)/shard_map/all_to_all | solution.py:229
  26.4 0.0 collective-permute-done.2.refs_3_
  26.4 0.0 collective-permute-done.3.refs_4_
  26.4 3.4 %collective-permute-start.4 = (f32[96,2048]{1,0:T(8,128)}, f32[96,2048]{1,0:T(8,128)}, u32[]{:S(2)}, u32[]{:S(2)}) collective-permute-start(f32[96,2048]{1,0:T(8,128)} %bitcast.refs_2_), channel_id=1, source_target_pairs={{0,32},{1,33},{64,96},{65,97},{128,160},{129,161},{192,224},{193,2... | collective-permute-start | bytes 2359304 | tf_op jit(solution)/shard_map/ppermute | solution.py:223
  29.9 3.8 %collective-permute-done.given = f32[72,512]{1,0:T(8,128)} collective-permute-done((f32[72,512]{1,0:T(8,128)}, f32[72,512]{1,0:T(8,128)}, u32[]{:S(2)}, u32[]{:S(2)}) %collective-permute-start) | collective-permute-done | bytes 147488 | tf_op jit(solution)/shard_map/ppermute | solution.py:223
  33.6 2.1 %spread_far.1 = f32[8,72,512]{2,1,0:T(8,128)} custom-call(f32[72,512]{1,0:T(8,128)} %collective-permute-done.given), custom_call_target="tpu_custom_call" | custom-call | flops 12000000000 | bytes 1327104 | tf_op jit(solution)/shard_map/spread_far/pallas_call | solution.py:177
  35.7 5.5 %all-to-all-done.1.refs_0_ = f32[4,144,512]{2,1,0:T(8,128)} async-done(((f32[4,144,512]{2,1,0:T(8,128)}), f32[4,144,512]{2,1,0:T(8,128)}, u32[]{:S(2)}, u32[]{:S(2)}) %all-to-all-start.1) | async-done | bytes 1179680 | tf_op jit(solution)/shard_map/all_to_all | solution.py:229
  41.3 3.6 %all-to-all-start = ((f32[8,72,512]{2,1,0:T(8,128)}), f32[8,72,512]{2,1,0:T(8,128)S(1)}, u32[]{:S(2)}, u32[]{:S(2)}) async-start(f32[8,72,512]{2,1,0:T(8,128)} %spread_far.1), calls=%async_computation | async-start | bytes 2359296 | tf_op jit(solution)/shard_map/all_to_all | solution.py:233
  44.8 4.8 %collective-permute-start.1 = (f32[4,144,512]{2,1,0:T(8,128)}, f32[4,144,512]{2,1,0:T(8,128)S(1)}, u32[]{:S(2)}, u32[]{:S(2)}) collective-permute-start(f32[4,144,512]{2,1,0:T(8,128)} %all-to-all-done.1.refs_0_), channel_id=1, source_target_pairs={{0,1},{1,0},{64,65},{65,64},{128,129},{129,128},{192,193},{193,192... | collective-permute-start | bytes 3538952 | tf_op jit(solution)/shard_map/ppermute | solution.py:223
  49.6 0.0 collective-permute-done.4.refs_0_.refs_5_
  49.6 2.6 %collective-permute-done.1.refs_1_ = f32[4,144,512]{2,1,0:T(8,128)S(1)} collective-permute-done((f32[4,144,512]{2,1,0:T(8,128)}, f32[4,144,512]{2,1,0:T(8,128)S(1)}, u32[]{:S(2)}, u32[]{:S(2)}) %collective-permute-start.1) | collective-permute-done | bytes 1179680 | tf_op jit(solution)/shard_map/ppermute | solution.py:223
  52.3 3.7 %ladder_near.1.refs_0_ = f32[4,144,384]{2,1,0:T(8,128)S(1)} custom-call(f32[4,144,512]{2,1,0:T(8,128)} %all-to-all-done.1.refs_0_, f32[4,144,512]{2,1,0:T(8,128)S(1)} %collective-permute-done.1.refs_1_, f32[96,2048]{1,0:T(8,128)} %bitcast.refs_2_, f32[96,2048]{1,0:T(8,128)} %collective-permute-done.2.refs_3_, f32[96,2048]{1,0:T(8,128)} %collective-permute-done.3.refs_4_, ...), custom_call_target="tpu_custom_call" | custom-call | flops 27179089920 | bytes 3932160 | tf_op jit(solution)/shard_map/ladder_near/pallas_call | solution.py:121
  55.9 1.3 %all-to-all-done.refs_1_ = f32[8,72,512]{2,1,0:T(8,128)S(1)} async-done(((f32[8,72,512]{2,1,0:T(8,128)}), f32[8,72,512]{2,1,0:T(8,128)S(1)}, u32[]{:S(2)}, u32[]{:S(2)}) %all-to-all-start) | async-done | bytes 1179680 | tf_op jit(solution)/shard_map/all_to_all | solution.py:233
  57.3 6.5 %collective-permute-start.5 = (f32[8,72,512]{2,1,0:T(8,128)S(1)}, f32[8,72,512]{2,1,0:T(8,128)S(1)}, u32[]{:S(2)}, u32[]{:S(2)}) collective-permute-start(f32[8,72,512]{2,1,0:T(8,128)S(1)} %all-to-all-done.refs_1_), channel_id=1, source_target_pairs={{0,1},{1,0},{64,65},{65,64},{128,129},{129,128},{192,193},{193,192... | collective-permute-start | bytes 3538952 | tf_op jit(solution)/shard_map/ppermute | solution.py:223
  63.8 2.5 %ladder_far.1.refs_0_ = f32[4,144,384]{2,1,0:T(8,128)S(1)} custom-call(f32[4,144,384]{2,1,0:T(8,128)S(1)} %ladder_near.1.refs_0_, f32[8,72,512]{2,1,0:T(8,128)S(1)} %all-to-all-done.refs_1_, f32[96,2048]{1,0:T(8,128)} %bitcast.refs_2_, f32[96,2048]{1,0:T(8,128)} %collective-permute-done.2.refs_3_, f32[96,2048]{1,0:T(8,128)} %collective-permute-done.3.refs_4_, ...), custom_call_target="tpu_custom_call" | custom-call | flops 679477248 | bytes 1966080 | tf_op jit(solution)/shard_map/ladder_far/pallas_call | solution.py:121
  66.3 0.0 collective-permute-done.5.refs_1_
  66.3 2.5 %ladder_far_pair.1 = f32[4,144,384]{2,1,0:T(8,128)S(1)} custom-call(f32[4,144,384]{2,1,0:T(8,128)S(1)} %ladder_far.1.refs_0_, f32[8,72,512]{2,1,0:T(8,128)S(1)} %collective-permute-done.5.refs_1_, f32[96,2048]{1,0:T(8,128)} %bitcast.refs_2_, f32[96,2048]{1,0:T(8,128)} %collective-permute-done.2.refs_3_, f32[96,2048]{1,0:T(8,128)} %collective-permute-done.3.refs_4_, ...), custom_call_target="tpu_custom_call" | custom-call | flops 679477248 | bytes 1966080 | tf_op jit(solution)/shard_map/ladder_far_pair/pallas_call | solution.py:121
  68.8 0.0 copy-start
  68.8 15.4 %all_to_all.15.parts = f32[4,144,384]{2,1,0:T(8,128)S(1)} all-to-all(f32[4,144,384]{2,1,0:T(8,128)S(1)} %ladder_far_pair.1), channel_id=1, replica_groups={{0,4,8,12},{16,20,24,28},{32,36,40,44},{48,52,56,60},{1,5,9,13},{17,21,..., dimensions={0} | all-to-all | bytes 1769472 | tf_op jit(solution)/shard_map/all_to_all | solution.py:244
  84.2 0.0 copy-done
  84.2 1.3 %add_ladder.1 = f32[144,1536]{1,0:T(8,128)} custom-call(f32[144,1536]{1,0:T(8,128)S(1)} %copy-done, f32[4,144,384]{2,1,0:T(8,128)S(1)} %all_to_all.15.parts), custom_call_target="tpu_custom_call" | custom-call | tf_op jit(solution)/shard_map/add_ladder/pallas_call | solution.py:208
  (1 shorter events, 0.0 us)
Async XLA Ops:
  0.0 26.4 %collective-permute-start.2 = (f32[96,2048]{1,0:T(8,128)}, f32[96,2048]{1,0:T(8,128)}, u32[]{:S(2)}, u32[]{:S(2)}) collective-permute-start(f32[96,2048]{1,0:T(8,128)} %bitcast.refs_2_), channel_id=1, source_target_pairs={{0,16},{1,17},{64,80},{65,81},{128,144},{129,145},{192,208},{193,2... | collective-permute-start | bytes 2359304 | tf_op jit(solution)/shard_map/ppermute | solution.py:223
  3.9 22.5 %collective-permute-start.3 = (f32[96,2048]{1,0:T(8,128)}, f32[96,2048]{1,0:T(8,128)}, u32[]{:S(2)}, u32[]{:S(2)}) collective-permute-start(f32[96,2048]{1,0:T(8,128)} %bitcast.refs_2_), channel_id=1, source_target_pairs={{0,48},{1,49},{64,112},{65,113},{128,176},{129,177},{192,240},{193... | collective-permute-start | bytes 2359304 | tf_op jit(solution)/shard_map/ppermute | solution.py:223
  8.7 24.9 %collective-permute-start = (f32[72,512]{1,0:T(8,128)}, f32[72,512]{1,0:T(8,128)}, u32[]{:S(2)}, u32[]{:S(2)}) collective-permute-start(f32[72,512]{1,0:T(8,128)} %constant_dynamic-slice_fusion), channel_id=1, source_target_pairs={{0,450},{1,451},{64,386},{65,387},{128,322},{129,323},{192,258},{1... | collective-permute-start | bytes 442376 | tf_op jit(solution)/shard_map/ppermute | solution.py:223
  22.1 19.1 %all-to-all-start.1 = ((f32[4,144,512]{2,1,0:T(8,128)}), f32[4,144,512]{2,1,0:T(8,128)}, u32[]{:S(2)}, u32[]{:S(2)}) async-start(f32[4,144,512]{2,1,0:T(8,128)} %spread_near.1), calls=%async_computation.1 | async-start | bytes 2359296 | tf_op jit(solution)/shard_map/all_to_all | solution.py:229
  26.4 23.2 %collective-permute-start.4 = (f32[96,2048]{1,0:T(8,128)}, f32[96,2048]{1,0:T(8,128)}, u32[]{:S(2)}, u32[]{:S(2)}) collective-permute-start(f32[96,2048]{1,0:T(8,128)} %bitcast.refs_2_), channel_id=1, source_target_pairs={{0,32},{1,33},{64,96},{65,97},{128,160},{129,161},{192,224},{193,2... | collective-permute-start | bytes 2359304 | tf_op jit(solution)/shard_map/ppermute | solution.py:223
  41.3 16.0 %all-to-all-start = ((f32[8,72,512]{2,1,0:T(8,128)}), f32[8,72,512]{2,1,0:T(8,128)S(1)}, u32[]{:S(2)}, u32[]{:S(2)}) async-start(f32[8,72,512]{2,1,0:T(8,128)} %spread_far.1), calls=%async_computation | async-start | bytes 2359296 | tf_op jit(solution)/shard_map/all_to_all | solution.py:233
  44.8 7.5 %collective-permute-start.1 = (f32[4,144,512]{2,1,0:T(8,128)}, f32[4,144,512]{2,1,0:T(8,128)S(1)}, u32[]{:S(2)}, u32[]{:S(2)}) collective-permute-start(f32[4,144,512]{2,1,0:T(8,128)} %all-to-all-done.1.refs_0_), channel_id=1, source_target_pairs={{0,1},{1,0},{64,65},{65,64},{128,129},{129,128},{192,193},{193,192... | collective-permute-start | bytes 3538952 | tf_op jit(solution)/shard_map/ppermute | solution.py:223
  57.3 9.0 %collective-permute-start.5 = (f32[8,72,512]{2,1,0:T(8,128)S(1)}, f32[8,72,512]{2,1,0:T(8,128)S(1)}, u32[]{:S(2)}, u32[]{:S(2)}) collective-permute-start(f32[8,72,512]{2,1,0:T(8,128)S(1)} %all-to-all-done.refs_1_), channel_id=1, source_target_pairs={{0,1},{1,0},{64,65},{65,64},{128,129},{129,128},{192,193},{193,192... | collective-permute-start | bytes 3538952 | tf_op jit(solution)/shard_map/ppermute | solution.py:223
  68.8 15.4 %copy-start = (f32[144,1536]{1,0:T(8,128)S(1)}, f32[144,1536]{1,0:T(8,128)}, u32[]{:S(2)}) copy-start(f32[144,1536]{1,0:T(8,128)} %residual.1) | copy-start | bytes 2654212

commit v5 on v3

--- a/solution.py
+++ b/solution.py
@@ -60,7 +60,7 @@
     if accumulate:
         so_far, refs = refs[0], refs[1:]
     terms, blocks, refs = refs[:n], refs[n : n + n_blocks], refs[n + n_blocks :]
-    own = 3 + accumulate * 2 + fetch * 2
+    own = 3 + fetch * 2
     out, v_ref, v_sems, *rest = refs[-own:]
     layer = lax.axis_index("layer")
     width = v_ref.shape[2]
@@ -77,8 +77,6 @@
             copies.append(pltpu.make_async_copy(block.at[:, at], taken, v_sems.at[k, m]))
             row += block.shape[0]
         waits.append(copies)
-    if accumulate:
-        waits.append([pltpu.make_async_copy(so_far, rest[0], rest[1])])
     for copies in waits:
         for copy in copies:
             copy.start()
@@ -97,8 +95,7 @@
         total = term if total is None else total + term
     total = total.reshape(out.shape)
     if accumulate:
-        waits[n][0].wait()
-        total = rest[0][...] + total
+        total = so_far[...] + total
     out[...] = total
 
 
@@ -111,8 +108,6 @@
         pltpu.VMEM((len(turns), columns, width), jnp.float32),
         pltpu.SemaphoreType.DMA((len(turns), len(blocks))),
     ]
-    if so_far is not None:
-        scratch += [pltpu.VMEM(shape, jnp.float32), pltpu.SemaphoreType.DMA]
     if fetch:
         scratch += [
             pltpu.VMEM((len(turns), *terms[0].shape), jnp.float32),
@@ -121,7 +116,7 @@
     return pl.pallas_call(
         functools.partial(ladder_kernel, turns, so_far is not None, fetch, len(blocks)),
         out_shape=jax.ShapeDtypeStruct(shape, jnp.float32),
-        in_specs=[there] * (so_far is not None)
+        in_specs=[here] * (so_far is not None)
         + [there if fetch else here] * len(terms)
         + [there] * (len(blocks) + len(after)),
         out_specs=here,

time: 86.5 us -> 86.4 us (level)
  transfers between devices with their start and end apart: 8 -> 8, of which waited for: 4 -> 5; matrix products, arithmetic and copies ran while one was open for 0% -> 0% of each run, Pallas kernels for 13% -> 13%
where the time goes in v5:
time: 86.4 us; the launch traced here: 85.6 us
  starting transfers between devices  41.1 us (48%)
  blocking collectives  15.4 us (18%)
  Pallas kernels  14.6 us (17%)
  waiting for transfers between devices  13.4 us (16%)
  local copies, waits for them, and re-layouts  0.96 us (1%)
    ppermute x6, starting transfers between devices, send(): return lax.ppermute(value, AXES, shifted(**move))  33.2 us
    all_to_all x1, blocking collectives, on_device(): parts = lax.all_to_all(total, 'col', 0, 0, axis_index_groups=Y_RINGS)  15.4 us
    pallas_call x3, Pallas kernels, ladder(): pl.pallas_call(functools.partial(ladder_kernel, turns, so_far is not None...  8.44 us
    ppermute x6, waiting for transfers between devices, send(): return lax.ppermute(value, AXES, shifted(**move))  6.5 us
    all_to_all x1, waiting for transfers between devices, on_device(): lax.all_to_all(spread(t, SIDE, 'spread_near'), 'col', 0, 0, axis_index_gr...  5.54 us
    all_to_all x1, starting transfers between devices, on_device(): lax.all_to_all(spread(t, SIDE, 'spread_near'), 'col', 0, 0, axis_index_gr...  4.27 us
    pallas_call x2, Pallas kernels, spread(): pl.pallas_call(spread_kernel, out_shape=jax.ShapeDtypeStruct((copies, *va...  4.05 us
    all_to_all x1, starting transfers between devices, on_device(): lax.all_to_all(far, ('row', 'col'), 0, 0, axis_index_groups=Y_RINGS_OF_TWO)  3.56 us
  transfers between devices with their start and end apart: 8, of which 5 were waited for; matrix products, arithmetic and copies ran while one was open for 0% of the time, Pallas kernels for 13%

profile of v5, /device:TPU:1, one launch (start us, length us, event | category | flops | bytes accessed | tf_op | source)
XLA Modules:
  0.0 85.6 jit_solution(11190435356290684020)
XLA Ops:
  0.0 3.9 %collective-permute-start.2 = (f32[96,2048]{1,0:T(8,128)}, f32[96,2048]{1,0:T(8,128)}, u32[]{:S(2)}, u32[]{:S(2)}) collective-permute-start(f32[96,2048]{1,0:T(8,128)} %bitcast.refs_2_), channel_id=1, source_target_pairs={{0,16},{1,17},{64,80},{65,81},{128,144},{129,145},{192,208},{193,2... | collective-permute-start | bytes 2359304 | tf_op jit(solution)/shard_map/ppermute | solution.py:230
  3.9 3.2 %collective-permute-start.3 = (f32[96,2048]{1,0:T(8,128)}, f32[96,2048]{1,0:T(8,128)}, u32[]{:S(2)}, u32[]{:S(2)}) collective-permute-start(f32[96,2048]{1,0:T(8,128)} %bitcast.refs_2_), channel_id=1, source_target_pairs={{0,48},{1,49},{64,112},{65,113},{128,176},{129,177},{192,240},{193... | collective-permute-start | bytes 2359304 | tf_op jit(solution)/shard_map/ppermute | solution.py:230
  7.1 0.0 copy-start
  7.2 1.0 %copy-done = f32[144,512]{1,0:T(8,128)S(1)} copy-done((f32[144,512]{1,0:T(8,128)S(1)}, f32[144,512]{1,0:T(8,128)}, u32[]{:S(2)}) %copy-start) | copy-done | bytes 294936
  8.1 0.8 share.1
  8.9 11.3 %collective-permute-start = (f32[72,512]{1,0:T(8,128)}, f32[72,512]{1,0:T(8,128)}, u32[]{:S(2)}, u32[]{:S(2)}) collective-permute-start(f32[72,512]{1,0:T(8,128)} %share.1), channel_id=1, source_target_pairs={{0,450},{1,451},{64,386},{65,387},{128,322},{129,323},{192,258},{1... | collective-permute-start | bytes 442376 | tf_op jit(solution)/shard_map/ppermute | solution.py:230
  20.3 2.0 %spread_near.1 = f32[4,144,512]{2,1,0:T(8,128)} custom-call(f32[144,512]{1,0:T(8,128)} %given.1), custom_call_target="tpu_custom_call" | custom-call | bytes 1474560 | tf_op jit(solution)/shard_map/spread_near/pallas_call | solution.py:162
  22.3 4.3 %all-to-all-start.1 = ((f32[4,144,512]{2,1,0:T(8,128)}), f32[4,144,512]{2,1,0:T(8,128)}, u32[]{:S(2)}, u32[]{:S(2)}) async-start(f32[4,144,512]{2,1,0:T(8,128)} %spread_near.1), calls=%async_computation.1 | async-start | bytes 2359296 | tf_op jit(solution)/shard_map/all_to_all | solution.py:234
  26.6 0.0 collective-permute-done.2.refs_3_
  26.6 0.0 collective-permute-done.3.refs_4_
  26.6 3.4 %collective-permute-start.4 = (f32[96,2048]{1,0:T(8,128)}, f32[96,2048]{1,0:T(8,128)}, u32[]{:S(2)}, u32[]{:S(2)}) collective-permute-start(f32[96,2048]{1,0:T(8,128)} %bitcast.refs_2_), channel_id=1, source_target_pairs={{0,32},{1,33},{64,96},{65,97},{128,160},{129,161},{192,224},{193,2... | collective-permute-start | bytes 2359304 | tf_op jit(solution)/shard_map/ppermute | solution.py:230
  30.1 3.8 %collective-permute-done.given = f32[72,512]{1,0:T(8,128)} collective-permute-done((f32[72,512]{1,0:T(8,128)}, f32[72,512]{1,0:T(8,128)}, u32[]{:S(2)}, u32[]{:S(2)}) %collective-permute-start) | collective-permute-done | bytes 147488 | tf_op jit(solution)/shard_map/ppermute | solution.py:230
  33.9 2.0 %spread_far.1 = f32[8,72,512]{2,1,0:T(8,128)} custom-call(f32[72,512]{1,0:T(8,128)} %collective-permute-done.given), custom_call_target="tpu_custom_call" | custom-call | flops 12000000000 | bytes 1327104 | tf_op jit(solution)/shard_map/spread_far/pallas_call | solution.py:162
  35.9 5.5 %all-to-all-done.1.refs_0_ = f32[4,144,512]{2,1,0:T(8,128)} async-done(((f32[4,144,512]{2,1,0:T(8,128)}), f32[4,144,512]{2,1,0:T(8,128)}, u32[]{:S(2)}, u32[]{:S(2)}) %all-to-all-start.1) | async-done | bytes 1179680 | tf_op jit(solution)/shard_map/all_to_all | solution.py:234
  41.4 3.6 %all-to-all-start = ((f32[8,72,512]{2,1,0:T(8,128)}), f32[8,72,512]{2,1,0:T(8,128)S(1)}, u32[]{:S(2)}, u32[]{:S(2)}) async-start(f32[8,72,512]{2,1,0:T(8,128)} %spread_far.1), calls=%async_computation | async-start | bytes 2359296 | tf_op jit(solution)/shard_map/all_to_all | solution.py:238
  45.0 4.8 %collective-permute-start.1 = (f32[4,144,512]{2,1,0:T(8,128)}, f32[4,144,512]{2,1,0:T(8,128)S(1)}, u32[]{:S(2)}, u32[]{:S(2)}) collective-permute-start(f32[4,144,512]{2,1,0:T(8,128)} %all-to-all-done.1.refs_0_), channel_id=1, source_target_pairs={{0,1},{1,0},{64,65},{65,64},{128,129},{129,128},{192,193},{193,192... | collective-permute-start | bytes 3538952 | tf_op jit(solution)/shard_map/ppermute | solution.py:230
  49.8 0.0 collective-permute-done.4.refs_0_.refs_5_
  49.8 2.6 %collective-permute-done.1.refs_1_ = f32[4,144,512]{2,1,0:T(8,128)S(1)} collective-permute-done((f32[4,144,512]{2,1,0:T(8,128)}, f32[4,144,512]{2,1,0:T(8,128)S(1)}, u32[]{:S(2)}, u32[]{:S(2)}) %collective-permute-start.1) | collective-permute-done | bytes 1179680 | tf_op jit(solution)/shard_map/ppermute | solution.py:230
  52.5 3.7 %ladder_near.1.refs_0_ = f32[4,144,384]{2,1,0:T(8,128)S(1)} custom-call(f32[4,144,512]{2,1,0:T(8,128)} %all-to-all-done.1.refs_0_, f32[4,144,512]{2,1,0:T(8,128)S(1)} %collective-permute-done.1.refs_1_, f32[96,2048]{1,0:T(8,128)} %bitcast.refs_2_, f32[96,2048]{1,0:T(8,128)} %collective-permute-done.2.refs_3_, f32[96,2048]{1,0:T(8,128)} %collective-permute-done.3.refs_4_, ...), custom_call_target="tpu_custom_call" | custom-call | flops 27179089920 | bytes 3932160 | tf_op jit(solution)/shard_map/ladder_near/pallas_call | solution.py:116
  56.1 1.3 %all-to-all-done.refs_1_ = f32[8,72,512]{2,1,0:T(8,128)S(1)} async-done(((f32[8,72,512]{2,1,0:T(8,128)}), f32[8,72,512]{2,1,0:T(8,128)S(1)}, u32[]{:S(2)}, u32[]{:S(2)}) %all-to-all-start) | async-done | bytes 1179680 | tf_op jit(solution)/shard_map/all_to_all | solution.py:238
  57.4 6.6 %collective-permute-start.5 = (f32[8,72,512]{2,1,0:T(8,128)S(1)}, f32[8,72,512]{2,1,0:T(8,128)S(1)}, u32[]{:S(2)}, u32[]{:S(2)}) collective-permute-start(f32[8,72,512]{2,1,0:T(8,128)S(1)} %all-to-all-done.refs_1_), channel_id=1, source_target_pairs={{0,1},{1,0},{64,65},{65,64},{128,129},{129,128},{192,193},{193,192... | collective-permute-start | bytes 3538952 | tf_op jit(solution)/shard_map/ppermute | solution.py:230
  64.0 2.4 %ladder_far.1.refs_0_ = f32[4,144,384]{2,1,0:T(8,128)S(1)} custom-call(f32[4,144,384]{2,1,0:T(8,128)S(1)} %ladder_near.1.refs_0_, f32[8,72,512]{2,1,0:T(8,128)S(1)} %all-to-all-done.refs_1_, f32[96,2048]{1,0:T(8,128)} %bitcast.refs_2_, f32[96,2048]{1,0:T(8,128)} %collective-permute-done.2.refs_3_, f32[96,2048]{1,0:T(8,128)} %collective-permute-done.3.refs_4_, ...), custom_call_target="tpu_custom_call" | custom-call | flops 679477248 | bytes 1966080 | tf_op jit(solution)/shard_map/ladder_far/pallas_call | solution.py:116
  66.4 0.1 collective-permute-done.5.refs_1_
  66.4 2.4 %ladder_far_pair.1 = f32[4,144,384]{2,1,0:T(8,128)S(1)} custom-call(f32[4,144,384]{2,1,0:T(8,128)S(1)} %ladder_far.1.refs_0_, f32[8,72,512]{2,1,0:T(8,128)S(1)} %collective-permute-done.5.refs_1_, f32[96,2048]{1,0:T(8,128)} %bitcast.refs_2_, f32[96,2048]{1,0:T(8,128)} %collective-permute-done.2.refs_3_, f32[96,2048]{1,0:T(8,128)} %collective-permute-done.3.refs_4_, ...), custom_call_target="tpu_custom_call" | custom-call | flops 679477248 | bytes 1966080 | tf_op jit(solution)/shard_map/ladder_far_pair/pallas_call | solution.py:116
  68.8 0.0 copy-start.1
  68.9 15.4 %all_to_all.15.parts = f32[4,144,384]{2,1,0:T(8,128)S(1)} all-to-all(f32[4,144,384]{2,1,0:T(8,128)S(1)} %ladder_far_pair.1), channel_id=1, replica_groups={{0,4,8,12},{16,20,24,28},{32,36,40,44},{48,52,56,60},{1,5,9,13},{17,21,..., dimensions={0} | all-to-all | bytes 1769472 | tf_op jit(solution)/shard_map/all_to_all | solution.py:249
  84.2 0.0 copy-done.1
  84.2 1.3 %add_ladder.1 = f32[144,1536]{1,0:T(8,128)} custom-call(f32[144,1536]{1,0:T(8,128)S(1)} %copy-done.1, f32[4,144,384]{2,1,0:T(8,128)S(1)} %all_to_all.15.parts), custom_call_target="tpu_custom_call" | custom-call | tf_op jit(solution)/shard_map/add_ladder/pallas_call | solution.py:215
  (1 shorter events, 0.0 us)
Async XLA Ops:
  0.0 26.6 %collective-permute-start.2 = (f32[96,2048]{1,0:T(8,128)}, f32[96,2048]{1,0:T(8,128)}, u32[]{:S(2)}, u32[]{:S(2)}) collective-permute-start(f32[96,2048]{1,0:T(8,128)} %bitcast.refs_2_), channel_id=1, source_target_pairs={{0,16},{1,17},{64,80},{65,81},{128,144},{129,145},{192,208},{193,2... | collective-permute-start | bytes 2359304 | tf_op jit(solution)/shard_map/ppermute | solution.py:230
  3.9 22.7 %collective-permute-start.3 = (f32[96,2048]{1,0:T(8,128)}, f32[96,2048]{1,0:T(8,128)}, u32[]{:S(2)}, u32[]{:S(2)}) collective-permute-start(f32[96,2048]{1,0:T(8,128)} %bitcast.refs_2_), channel_id=1, source_target_pairs={{0,48},{1,49},{64,112},{65,113},{128,176},{129,177},{192,240},{193... | collective-permute-start | bytes 2359304 | tf_op jit(solution)/shard_map/ppermute | solution.py:230
  7.1 1.0 %copy-start = (f32[144,512]{1,0:T(8,128)S(1)}, f32[144,512]{1,0:T(8,128)}, u32[]{:S(2)}) copy-start(f32[144,512]{1,0:T(8,128)} %given.1) | copy-start | bytes 884740
  8.9 24.9 %collective-permute-start = (f32[72,512]{1,0:T(8,128)}, f32[72,512]{1,0:T(8,128)}, u32[]{:S(2)}, u32[]{:S(2)}) collective-permute-start(f32[72,512]{1,0:T(8,128)} %share.1), channel_id=1, source_target_pairs={{0,450},{1,451},{64,386},{65,387},{128,322},{129,323},{192,258},{1... | collective-permute-start | bytes 442376 | tf_op jit(solution)/shard_map/ppermute | solution.py:230
  22.3 19.1 %all-to-all-start.1 = ((f32[4,144,512]{2,1,0:T(8,128)}), f32[4,144,512]{2,1,0:T(8,128)}, u32[]{:S(2)}, u32[]{:S(2)}) async-start(f32[4,144,512]{2,1,0:T(8,128)} %spread_near.1), calls=%async_computation.1 | async-start | bytes 2359296 | tf_op jit(solution)/shard_map/all_to_all | solution.py:234
  26.6 23.2 %collective-permute-start.4 = (f32[96,2048]{1,0:T(8,128)}, f32[96,2048]{1,0:T(8,128)}, u32[]{:S(2)}, u32[]{:S(2)}) collective-permute-start(f32[96,2048]{1,0:T(8,128)} %bitcast.refs_2_), channel_id=1, source_target_pairs={{0,32},{1,33},{64,96},{65,97},{128,160},{129,161},{192,224},{193,2... | collective-permute-start | bytes 2359304 | tf_op jit(solution)/shard_map/ppermute | solution.py:230
  41.4 16.0 %all-to-all-start = ((f32[8,72,512]{2,1,0:T(8,128)}), f32[8,72,512]{2,1,0:T(8,128)S(1)}, u32[]{:S(2)}, u32[]{:S(2)}) async-start(f32[8,72,512]{2,1,0:T(8,128)} %spread_far.1), calls=%async_computation | async-start | bytes 2359296 | tf_op jit(solution)/shard_map/all_to_all | solution.py:238
  45.0 7.5 %collective-permute-start.1 = (f32[4,144,512]{2,1,0:T(8,128)}, f32[4,144,512]{2,1,0:T(8,128)S(1)}, u32[]{:S(2)}, u32[]{:S(2)}) collective-permute-start(f32[4,144,512]{2,1,0:T(8,128)} %all-to-all-done.1.refs_0_), channel_id=1, source_target_pairs={{0,1},{1,0},{64,65},{65,64},{128,129},{129,128},{192,193},{193,192... | collective-permute-start | bytes 3538952 | tf_op jit(solution)/shard_map/ppermute | solution.py:230
  57.4 9.0 %collective-permute-start.5 = (f32[8,72,512]{2,1,0:T(8,128)S(1)}, f32[8,72,512]{2,1,0:T(8,128)S(1)}, u32[]{:S(2)}, u32[]{:S(2)}) collective-permute-start(f32[8,72,512]{2,1,0:T(8,128)S(1)} %all-to-all-done.refs_1_), channel_id=1, source_target_pairs={{0,1},{1,0},{64,65},{65,64},{128,129},{129,128},{192,193},{193,192... | collective-permute-start | bytes 3538952 | tf_op jit(solution)/shard_map/ppermute | solution.py:230
  68.8 15.4 %copy-start.1 = (f32[144,1536]{1,0:T(8,128)S(1)}, f32[144,1536]{1,0:T(8,128)}, u32[]{:S(2)}) copy-start(f32[144,1536]{1,0:T(8,128)} %residual.1) | copy-start | bytes 2654212

commit v6 on v5

--- a/solution.py
+++ b/solution.py
@@ -177,28 +177,6 @@
     )(value)
 
 
-def share_kernel(t, out, sem):
-    rows = out.shape[0]
-    at = pl.ds(pl.multiple_of((1 - lax.axis_index("row") % 2) * rows, 8), rows)
-    copy = pltpu.make_async_copy(t.at[at], out, sem)
-    copy.start()
-    copy.wait()
-
-
-def share_of(t):
-    rows, width = t.shape
-    return pl.pallas_call(
-        share_kernel,
-        out_shape=jax.ShapeDtypeStruct((rows // 2, width), jnp.float32),
-        in_specs=[pl.BlockSpec(memory_space=pl.ANY)],
-        out_specs=pl.BlockSpec(memory_space=pltpu.VMEM),
-        scratch_shapes=[pltpu.SemaphoreType.DMA],
-        cost_estimate=pl.CostEstimate(flops=0, bytes_accessed=4 * t.size, transcendentals=0),
-        compiler_params=pltpu.CompilerParams(vmem_limit_bytes=LIMIT),
-        name="share",
-    )(t)
-
-
 def add_kernel(order, residual, parts, out):
     x = lax.axis_index("col") // SIDE
     ys, _, columns = parts.shape
@@ -229,7 +207,9 @@
     def send(value, **move):
         return lax.ppermute(value, AXES, shifted(**move))
 
-    share_far = send(share_of(t), mirror=True)
+    half = rows // 2
+    share = lax.dynamic_slice_in_dim(t, (1 - lax.axis_index("row") % 2) * half, half, 0)
+    share_far = send(share, mirror=True)
     v_left, v_right = send(v, dx=1), send(v, dx=-1)
     near = lax.all_to_all(spread(t, SIDE, "spread_near"), "col", 0, 0, axis_index_groups=Y_RINGS)
     v_left, v_right, v_next = lax.optimization_barrier((v_left, v_right, v))

time: 86.4 us -> 86.1 us (level)
    dynamic_slice x0 -> x1, local copies, waits for them, and re-layouts: none -> 1.59 us  [on_device(): lax.dynamic_slice_in_dim(t, (1 - lax.axis_index('row') % 2) * half, half, 0)]
    unnamed x4 -> x2, local copies, waits for them, and re-layouts: 0.96 us -> 0.01 us
  transfers between devices with their start and end apart: 8 -> 8, of which waited for: 5 -> 5; matrix products, arithmetic and copies ran while one was open for 0% -> 2% of each run, Pallas kernels for 13% -> 12%
where the time goes in v6:
time: 86.1 us; the launch traced here: 85.4 us
  starting transfers between devices  41 us (48%)
  blocking collectives  15.4 us (18%)
  Pallas kernels  13.8 us (16%)
  waiting for transfers between devices  13.4 us (16%)
  local copies, waits for them, and re-layouts  1.59 us (2%)
    ppermute x6, starting transfers between devices, send(): return lax.ppermute(value, AXES, shifted(**move))  33.2 us
    all_to_all x1, blocking collectives, on_device(): parts = lax.all_to_all(total, 'col', 0, 0, axis_index_groups=Y_RINGS)  15.4 us
    pallas_call x3, Pallas kernels, ladder(): pl.pallas_call(functools.partial(ladder_kernel, turns, so_far is not None...  8.43 us
    ppermute x6, waiting for transfers between devices, send(): return lax.ppermute(value, AXES, shifted(**move))  6.48 us
    all_to_all x1, waiting for transfers between devices, on_device(): lax.all_to_all(spread(t, SIDE, 'spread_near'), 'col', 0, 0, axis_index_gr...  5.56 us
    all_to_all x1, starting transfers between devices, on_device(): lax.all_to_all(spread(t, SIDE, 'spread_near'), 'col', 0, 0, axis_index_gr...  4.28 us
    pallas_call x2, Pallas kernels, spread(): pl.pallas_call(spread_kernel, out_shape=jax.ShapeDtypeStruct((copies, *va...  4.06 us
    all_to_all x1, starting transfers between devices, on_device(): lax.all_to_all(far, ('row', 'col'), 0, 0, axis_index_groups=Y_RINGS_OF_TWO)  3.56 us
  transfers between devices with their start and end apart: 8, of which 5 were waited for; matrix products, arithmetic and copies ran while one was open for 2% of the time, Pallas kernels for 12%

profile of v6, /device:TPU:1, one launch (start us, length us, event | category | flops | bytes accessed | tf_op | source)
XLA Modules:
  0.0 85.4 jit_solution(2961183392251092109)
XLA Ops:
  0.0 3.9 %collective-permute-start.2 = (f32[96,2048]{1,0:T(8,128)}, f32[96,2048]{1,0:T(8,128)}, u32[]{:S(2)}, u32[]{:S(2)}) collective-permute-start(f32[96,2048]{1,0:T(8,128)} %bitcast.refs_2_), channel_id=1, source_target_pairs={{0,16},{1,17},{64,80},{65,81},{128,144},{129,145},{192,208},{193,2... | collective-permute-start | bytes 2359304 | tf_op jit(solution)/shard_map/ppermute | solution.py:208
  3.9 3.2 %collective-permute-start.3 = (f32[96,2048]{1,0:T(8,128)}, f32[96,2048]{1,0:T(8,128)}, u32[]{:S(2)}, u32[]{:S(2)}) collective-permute-start(f32[96,2048]{1,0:T(8,128)} %bitcast.refs_2_), channel_id=1, source_target_pairs={{0,48},{1,49},{64,112},{65,113},{128,176},{129,177},{192,240},{193... | collective-permute-start | bytes 2359304 | tf_op jit(solution)/shard_map/ppermute | solution.py:208
  7.2 1.6 %constant_dynamic-slice_fusion = f32[72,512]{1,0:T(8,128)} fusion(f32[144,512]{1,0:T(8,128)} %given.1, s32[]{:T(128)S(6)} %select_n.11), kind=kLoop, calls=%fused_computation | loop fusion | bytes 294916 | tf_op jit(solution)/shard_map/dynamic_slice | solution.py:211
  8.7 11.3 %collective-permute-start = (f32[72,512]{1,0:T(8,128)}, f32[72,512]{1,0:T(8,128)}, u32[]{:S(2)}, u32[]{:S(2)}) collective-permute-start(f32[72,512]{1,0:T(8,128)} %constant_dynamic-slice_fusion), channel_id=1, source_target_pairs={{0,450},{1,451},{64,386},{65,387},{128,322},{129,323},{192,258},{1... | collective-permute-start | bytes 442376 | tf_op jit(solution)/shard_map/ppermute | solution.py:208
  20.1 2.0 %spread_near.1 = f32[4,144,512]{2,1,0:T(8,128)} custom-call(f32[144,512]{1,0:T(8,128)} %given.1), custom_call_target="tpu_custom_call" | custom-call | bytes 1474560 | tf_op jit(solution)/shard_map/spread_near/pallas_call | solution.py:162
  22.1 4.3 %all-to-all-start.1 = ((f32[4,144,512]{2,1,0:T(8,128)}), f32[4,144,512]{2,1,0:T(8,128)}, u32[]{:S(2)}, u32[]{:S(2)}) async-start(f32[4,144,512]{2,1,0:T(8,128)} %spread_near.1), calls=%async_computation.1 | async-start | bytes 2359296 | tf_op jit(solution)/shard_map/all_to_all | solution.py:214
  26.4 0.0 collective-permute-done.2.refs_3_
  26.4 0.0 collective-permute-done.3.refs_4_
  26.4 3.4 %collective-permute-start.4 = (f32[96,2048]{1,0:T(8,128)}, f32[96,2048]{1,0:T(8,128)}, u32[]{:S(2)}, u32[]{:S(2)}) collective-permute-start(f32[96,2048]{1,0:T(8,128)} %bitcast.refs_2_), channel_id=1, source_target_pairs={{0,32},{1,33},{64,96},{65,97},{128,160},{129,161},{192,224},{193,2... | collective-permute-start | bytes 2359304 | tf_op jit(solution)/shard_map/ppermute | solution.py:208
  29.9 3.8 %collective-permute-done.given = f32[72,512]{1,0:T(8,128)} collective-permute-done((f32[72,512]{1,0:T(8,128)}, f32[72,512]{1,0:T(8,128)}, u32[]{:S(2)}, u32[]{:S(2)}) %collective-permute-start) | collective-permute-done | bytes 147488 | tf_op jit(solution)/shard_map/ppermute | solution.py:208
  33.6 2.0 %spread_far.1 = f32[8,72,512]{2,1,0:T(8,128)} custom-call(f32[72,512]{1,0:T(8,128)} %collective-permute-done.given), custom_call_target="tpu_custom_call" | custom-call | flops 12000000000 | bytes 1327104 | tf_op jit(solution)/shard_map/spread_far/pallas_call | solution.py:162
  35.7 5.6 %all-to-all-done.1.refs_0_ = f32[4,144,512]{2,1,0:T(8,128)} async-done(((f32[4,144,512]{2,1,0:T(8,128)}), f32[4,144,512]{2,1,0:T(8,128)}, u32[]{:S(2)}, u32[]{:S(2)}) %all-to-all-start.1) | async-done | bytes 1179680 | tf_op jit(solution)/shard_map/all_to_all | solution.py:214
  41.2 3.6 %all-to-all-start = ((f32[8,72,512]{2,1,0:T(8,128)}), f32[8,72,512]{2,1,0:T(8,128)S(1)}, u32[]{:S(2)}, u32[]{:S(2)}) async-start(f32[8,72,512]{2,1,0:T(8,128)} %spread_far.1), calls=%async_computation | async-start | bytes 2359296 | tf_op jit(solution)/shard_map/all_to_all | solution.py:218
  44.8 4.8 %collective-permute-start.1 = (f32[4,144,512]{2,1,0:T(8,128)}, f32[4,144,512]{2,1,0:T(8,128)S(1)}, u32[]{:S(2)}, u32[]{:S(2)}) collective-permute-start(f32[4,144,512]{2,1,0:T(8,128)} %all-to-all-done.1.refs_0_), channel_id=1, source_target_pairs={{0,1},{1,0},{64,65},{65,64},{128,129},{129,128},{192,193},{193,192... | collective-permute-start | bytes 3538952 | tf_op jit(solution)/shard_map/ppermute | solution.py:208
  49.6 0.0 collective-permute-done.4.refs_0_.refs_5_
  49.6 2.6 %collective-permute-done.1.refs_1_ = f32[4,144,512]{2,1,0:T(8,128)S(1)} collective-permute-done((f32[4,144,512]{2,1,0:T(8,128)}, f32[4,144,512]{2,1,0:T(8,128)S(1)}, u32[]{:S(2)}, u32[]{:S(2)}) %collective-permute-start.1) | collective-permute-done | bytes 1179680 | tf_op jit(solution)/shard_map/ppermute | solution.py:208
  52.3 3.7 %ladder_near.1.refs_0_ = f32[4,144,384]{2,1,0:T(8,128)S(1)} custom-call(f32[4,144,512]{2,1,0:T(8,128)} %all-to-all-done.1.refs_0_, f32[4,144,512]{2,1,0:T(8,128)S(1)} %collective-permute-done.1.refs_1_, f32[96,2048]{1,0:T(8,128)} %bitcast.refs_2_, f32[96,2048]{1,0:T(8,128)} %collective-permute-done.2.refs_3_, f32[96,2048]{1,0:T(8,128)} %collective-permute-done.3.refs_4_, ...), custom_call_target="tpu_custom_call" | custom-call | flops 27179089920 | bytes 3932160 | tf_op jit(solution)/shard_map/ladder_near/pallas_call | solution.py:116
  55.9 1.3 %all-to-all-done.refs_1_ = f32[8,72,512]{2,1,0:T(8,128)S(1)} async-done(((f32[8,72,512]{2,1,0:T(8,128)}), f32[8,72,512]{2,1,0:T(8,128)S(1)}, u32[]{:S(2)}, u32[]{:S(2)}) %all-to-all-start) | async-done | bytes 1179680 | tf_op jit(solution)/shard_map/all_to_all | solution.py:218
  57.2 6.5 %collective-permute-start.5 = (f32[8,72,512]{2,1,0:T(8,128)S(1)}, f32[8,72,512]{2,1,0:T(8,128)S(1)}, u32[]{:S(2)}, u32[]{:S(2)}) collective-permute-start(f32[8,72,512]{2,1,0:T(8,128)S(1)} %all-to-all-done.refs_1_), channel_id=1, source_target_pairs={{0,1},{1,0},{64,65},{65,64},{128,129},{129,128},{192,193},{193,192... | collective-permute-start | bytes 3538952 | tf_op jit(solution)/shard_map/ppermute | solution.py:208
  63.8 2.4 %ladder_far.1.refs_0_ = f32[4,144,384]{2,1,0:T(8,128)S(1)} custom-call(f32[4,144,384]{2,1,0:T(8,128)S(1)} %ladder_near.1.refs_0_, f32[8,72,512]{2,1,0:T(8,128)S(1)} %all-to-all-done.refs_1_, f32[96,2048]{1,0:T(8,128)} %bitcast.refs_2_, f32[96,2048]{1,0:T(8,128)} %collective-permute-done.2.refs_3_, f32[96,2048]{1,0:T(8,128)} %collective-permute-done.3.refs_4_, ...), custom_call_target="tpu_custom_call" | custom-call | flops 679477248 | bytes 1966080 | tf_op jit(solution)/shard_map/ladder_far/pallas_call | solution.py:116
  66.2 0.1 collective-permute-done.5.refs_1_
  66.3 2.4 %ladder_far_pair.1 = f32[4,144,384]{2,1,0:T(8,128)S(1)} custom-call(f32[4,144,384]{2,1,0:T(8,128)S(1)} %ladder_far.1.refs_0_, f32[8,72,512]{2,1,0:T(8,128)S(1)} %collective-permute-done.5.refs_1_, f32[96,2048]{1,0:T(8,128)} %bitcast.refs_2_, f32[96,2048]{1,0:T(8,128)} %collective-permute-done.2.refs_3_, f32[96,2048]{1,0:T(8,128)} %collective-permute-done.3.refs_4_, ...), custom_call_target="tpu_custom_call" | custom-call | flops 679477248 | bytes 1966080 | tf_op jit(solution)/shard_map/ladder_far_pair/pallas_call | solution.py:116
  68.6 0.0 copy-start
  68.7 15.4 %all_to_all.15.parts = f32[4,144,384]{2,1,0:T(8,128)S(1)} all-to-all(f32[4,144,384]{2,1,0:T(8,128)S(1)} %ladder_far_pair.1), channel_id=1, replica_groups={{0,4,8,12},{16,20,24,28},{32,36,40,44},{48,52,56,60},{1,5,9,13},{17,21,..., dimensions={0} | all-to-all | bytes 1769472 | tf_op jit(solution)/shard_map/all_to_all | solution.py:229
  84.0 0.0 copy-done
  84.0 1.3 %add_ladder.1 = f32[144,1536]{1,0:T(8,128)} custom-call(f32[144,1536]{1,0:T(8,128)S(1)} %copy-done, f32[4,144,384]{2,1,0:T(8,128)S(1)} %all_to_all.15.parts), custom_call_target="tpu_custom_call" | custom-call | tf_op jit(solution)/shard_map/add_ladder/pallas_call | solution.py:193
  (1 shorter events, 0.0 us)
Async XLA Ops:
  0.0 26.4 %collective-permute-start.2 = (f32[96,2048]{1,0:T(8,128)}, f32[96,2048]{1,0:T(8,128)}, u32[]{:S(2)}, u32[]{:S(2)}) collective-permute-start(f32[96,2048]{1,0:T(8,128)} %bitcast.refs_2_), channel_id=1, source_target_pairs={{0,16},{1,17},{64,80},{65,81},{128,144},{129,145},{192,208},{193,2... | collective-permute-start | bytes 2359304 | tf_op jit(solution)/shard_map/ppermute | solution.py:208
  3.9 22.5 %collective-permute-start.3 = (f32[96,2048]{1,0:T(8,128)}, f32[96,2048]{1,0:T(8,128)}, u32[]{:S(2)}, u32[]{:S(2)}) collective-permute-start(f32[96,2048]{1,0:T(8,128)} %bitcast.refs_2_), channel_id=1, source_target_pairs={{0,48},{1,49},{64,112},{65,113},{128,176},{129,177},{192,240},{193... | collective-permute-start | bytes 2359304 | tf_op jit(solution)/shard_map/ppermute | solution.py:208
  8.7 24.9 %collective-permute-start = (f32[72,512]{1,0:T(8,128)}, f32[72,512]{1,0:T(8,128)}, u32[]{:S(2)}, u32[]{:S(2)}) collective-permute-start(f32[72,512]{1,0:T(8,128)} %constant_dynamic-slice_fusion), channel_id=1, source_target_pairs={{0,450},{1,451},{64,386},{65,387},{128,322},{129,323},{192,258},{1... | collective-permute-start | bytes 442376 | tf_op jit(solution)/shard_map/ppermute | solution.py:208
  22.1 19.1 %all-to-all-start.1 = ((f32[4,144,512]{2,1,0:T(8,128)}), f32[4,144,512]{2,1,0:T(8,128)}, u32[]{:S(2)}, u32[]{:S(2)}) async-start(f32[4,144,512]{2,1,0:T(8,128)} %spread_near.1), calls=%async_computation.1 | async-start | bytes 2359296 | tf_op jit(solution)/shard_map/all_to_all | solution.py:214
  26.4 23.2 %collective-permute-start.4 = (f32[96,2048]{1,0:T(8,128)}, f32[96,2048]{1,0:T(8,128)}, u32[]{:S(2)}, u32[]{:S(2)}) collective-permute-start(f32[96,2048]{1,0:T(8,128)} %bitcast.refs_2_), channel_id=1, source_target_pairs={{0,32},{1,33},{64,96},{65,97},{128,160},{129,161},{192,224},{193,2... | collective-permute-start | bytes 2359304 | tf_op jit(solution)/shard_map/ppermute | solution.py:208
  41.2 16.0 %all-to-all-start = ((f32[8,72,512]{2,1,0:T(8,128)}), f32[8,72,512]{2,1,0:T(8,128)S(1)}, u32[]{:S(2)}, u32[]{:S(2)}) async-start(f32[8,72,512]{2,1,0:T(8,128)} %spread_far.1), calls=%async_computation | async-start | bytes 2359296 | tf_op jit(solution)/shard_map/all_to_all | solution.py:218
  44.8 7.5 %collective-permute-start.1 = (f32[4,144,512]{2,1,0:T(8,128)}, f32[4,144,512]{2,1,0:T(8,128)S(1)}, u32[]{:S(2)}, u32[]{:S(2)}) collective-permute-start(f32[4,144,512]{2,1,0:T(8,128)} %all-to-all-done.1.refs_0_), channel_id=1, source_target_pairs={{0,1},{1,0},{64,65},{65,64},{128,129},{129,128},{192,193},{193,192... | collective-permute-start | bytes 3538952 | tf_op jit(solution)/shard_map/ppermute | solution.py:208
  57.2 9.0 %collective-permute-start.5 = (f32[8,72,512]{2,1,0:T(8,128)S(1)}, f32[8,72,512]{2,1,0:T(8,128)S(1)}, u32[]{:S(2)}, u32[]{:S(2)}) collective-permute-start(f32[8,72,512]{2,1,0:T(8,128)S(1)} %all-to-all-done.refs_1_), channel_id=1, source_target_pairs={{0,1},{1,0},{64,65},{65,64},{128,129},{129,128},{192,193},{193,192... | collective-permute-start | bytes 3538952 | tf_op jit(solution)/shard_map/ppermute | solution.py:208
  68.6 15.4 %copy-start = (f32[144,1536]{1,0:T(8,128)S(1)}, f32[144,1536]{1,0:T(8,128)}, u32[]{:S(2)}) copy-start(f32[144,1536]{1,0:T(8,128)} %residual.1) | copy-start | bytes 2654212
